TPU v7x, 128 devices: a whole 4x4x4 slice. The times are simulated.
128 devices in a mesh: dp: 8 (over x, core), sy: 4 (over z), sx: 4 (over y).
Axes of the slice: x: 4, y: 4, z: 4, core: 2. Of those that a mesh axis runs over, the one named last changes fastest.
Arguments:
- features: bfloat16 [8, 64, 256, 768], P('dp', 'sy', 'sx'), may hold values from -100 to 100
- depth_weight: float32 [7, 7, 768], replicated, may hold values from -0.875 to 0.875
- depth_bias: float32 [768], replicated, may hold values from -3 to 3
- reduce_weight: bfloat16 [768, 256], replicated, may hold values from -0.21875 to 0.21875
- reduce_bias: float32 [256], replicated, may hold values from -3 to 3
- class_weight: bfloat16 [10, 256, 256], replicated, may hold values from -0.375 to 0.375
- class_bias: float32 [10], replicated, may hold values from -4 to 4
- labels: int32 [8], P('dp'), may hold values from 0 to 9
Outputs:
- loss: float32 [], replicated
- depth_weight_grad: float32 [7, 7, 768], replicated
- depth_bias_grad: float32 [768], replicated
- reduce_weight_grad: float32 [768, 256], replicated
- reduce_bias_grad: float32 [256], replicated
- class_weight_grad: float32 [10, 256, 256], replicated
- class_bias_grad: float32 [10], replicated
All inputs are finite; a program needn't handle non-finite values.
Results may differ from a plain program's by a relative error of at most 0.006.
Values may be sent and summed in bfloat16 or wider, within the bound.
A program may use at most 64 MiB of HBM per device.

v0:
```python
import jax
import jax.numpy as jnp
from jax import lax
from jax.sharding import PartitionSpec as P

KERNEL = 7
NEWTON_STEPS = 5


epsilon = 1e-05
loss_scale = 64.0
highest = lax.Precision.HIGHEST


def with_halo(block, sides, width):
    for axis, dim in sides:
        count = lax.axis_size(axis)
        forward = [(i, i + 1) for i in range(count - 1)]
        backward = [(target, source) for source, target in forward]
        low = lax.ppermute(
            lax.slice_in_dim(block, block.shape[dim] - width, None, axis=dim), axis, forward
        )
        high = lax.ppermute(lax.slice_in_dim(block, 0, width, axis=dim), axis, backward)
        block = jnp.concatenate([low, block, high], axis=dim)
    return block


def matrix_root(sigma):
    identity = jnp.eye(sigma.shape[0], dtype=sigma.dtype)
    trace_value = jnp.trace(sigma) + epsilon
    current = sigma / trace_value
    inverse = identity
    for iteration in range(NEWTON_STEPS):
        factor = 0.5 * (3.0 * identity - jnp.dot(inverse, current, precision=highest))
        current = jnp.dot(current, factor, precision=highest)
        inverse = jnp.dot(factor, inverse, precision=highest)
    return jnp.sqrt(trace_value) * current


def taps_conv(padded, tile_rows, tile_cols, depth_weight, depth_bias):
    total = jnp.zeros((tile_rows, tile_cols, padded.shape[2]), depth_weight.dtype) + depth_bias
    for row_tap in range(KERNEL):
        for col_tap in range(KERNEL):
            window = padded[row_tap : row_tap + tile_rows, col_tap : col_tap + tile_cols, :]
            total = total + window.astype(depth_weight.dtype) * depth_weight[row_tap, col_tap]
    return total.astype(jnp.bfloat16)


def body(
    features, depth_weight, depth_bias, reduce_weight, reduce_bias, class_weight, class_bias, labels
):
    tile_rows, tile_cols = (features.shape[1], features.shape[2])
    padded = with_halo(features, (("sy", 1), ("sx", 2)), KERNEL // 2)[0]
    conv_out = taps_conv(padded, tile_rows, tile_cols, depth_weight, depth_bias)
    flat_conv = conv_out.reshape(tile_rows * tile_cols, -1)
    before = jnp.dot(flat_conv, reduce_weight, preferred_element_type=jnp.float32) + reduce_bias
    feat = jax.nn.silu(before).astype(jnp.bfloat16)
    gram = lax.dot_general(feat, feat, (((0,), (0,)), ((), ())), preferred_element_type=jnp.float32)
    colsum = jnp.sum(feat.astype(jnp.float32), axis=0)
    gram, colsum = lax.psum((gram, colsum), ("sy", "sx"))
    count = tile_rows * tile_cols * lax.axis_size("sy") * lax.axis_size("sx")
    image_count = features.shape[0] * lax.axis_size("dp")
    mean_vec = colsum / count
    sigma = gram / count - jnp.outer(mean_vec, mean_vec)
    root, pullback = jax.vjp(matrix_root, sigma)
    weight_full = class_weight.astype(jnp.float32)
    logits = jnp.einsum("kij,ij->k", weight_full, root, precision=highest) + class_bias
    onehot = (jnp.arange(logits.shape[0], dtype=jnp.int32) == labels[0]).astype(jnp.float32)
    loss_part = jnp.sum(jax.nn.softplus(logits)) - jnp.sum(onehot * logits)
    logit_grad = loss_scale * (jax.nn.sigmoid(logits) - onehot) / image_count
    root_grad = jnp.einsum("k,kij->ij", logit_grad, weight_full, precision=highest)
    sigma_grad = pullback(root_grad)[0]
    class_local = logit_grad[:, None, None] * root[None, :, :]
    loss_total, class_weight_grad, class_bias_grad = lax.psum(
        (loss_part, class_local, logit_grad), "dp"
    )
    loss = loss_total / image_count
    symmetric = ((sigma_grad + sigma_grad.T) / count).astype(jnp.bfloat16)
    mean_term = jnp.dot(mean_vec, symmetric.astype(jnp.float32), precision=highest)
    feat_grad = jnp.dot(feat, symmetric, preferred_element_type=jnp.float32) - mean_term
    gate = jax.nn.sigmoid(before)
    pre_grad = (feat_grad * gate * (1.0 + before * (1.0 - gate))).astype(jnp.bfloat16)
    weight_grad = lax.dot_general(
        flat_conv, pre_grad, (((0,), (0,)), ((), ())), preferred_element_type=jnp.float32
    )
    bias_grad = jnp.sum(pre_grad.astype(jnp.float32), axis=0)
    conv_grad = lax.dot_general(
        pre_grad, reduce_weight, (((1,), (1,)), ((), ())), preferred_element_type=jnp.float32
    )
    conv_grad = conv_grad.astype(jnp.bfloat16).reshape(tile_rows, tile_cols, -1)
    depth_rows = []
    for row_tap in range(KERNEL):
        depth_cols = []
        for col_tap in range(KERNEL):
            window = padded[row_tap : row_tap + tile_rows, col_tap : col_tap + tile_cols, :]
            depth_cols.append(
                jnp.sum(window.astype(jnp.float32) * conv_grad.astype(jnp.float32), axis=(0, 1))
            )
        depth_rows.append(jnp.stack(depth_cols))
    depth_grad = jnp.stack(depth_rows)
    depth_bias_grad = jnp.sum(conv_grad.astype(jnp.float32), axis=(0, 1))
    weight_grad, depth_grad, depth_bias_grad, bias_grad = lax.psum(
        (weight_grad, depth_grad, depth_bias_grad, bias_grad), ("dp", "sy", "sx")
    )
    return (
        loss,
        depth_grad,
        depth_bias_grad,
        weight_grad,
        bias_grad,
        class_weight_grad,
        class_bias_grad,
    )


def solution(mesh):
    placed = (P("dp", "sy", "sx", None), P(), P(), P(), P(), P(), P(), P("dp"))
    return jax.shard_map(
        body,
        mesh=mesh,
        in_specs=placed,
        out_specs=(P(), P(), P(), P(), P(), P(), P()),
        check_vma=False,
    )
```

profile of v0, /device:TPU:1, one launch (start us, length us, event | category | flops | bytes accessed | tf_op | source)
XLA Modules:
  0.0 442.3 jit_solution(14651695696346182245)
XLA Ops:
  7.2 1.2 fusion.145
  8.4 4.4 collective-permute-start
  12.8 1.3 collective-permute-start.1
  14.1 1.4 slice_reduce_fusion.47
  15.5 1.4 slice_reduce_fusion.48
  16.9 1.6 collective-permute-done
  18.5 1.5 constant_dynamic-update-slice_fusion.1
  20.0 2.6 collective-permute-done.1
  22.8 3.2 collective-permute-start.2
  26.0 1.3 collective-permute-start.3
  27.3 1.1 slice_reduce_fusion.46
  28.4 3.4 collective-permute-done.3
  31.7 1.5 maximum_bitcast_fusion
  33.3 23.6 %fusion.98 = bf16[16,64,768]{2,1,0:T(8,128)(2,1)S(1)} fusion(f32[768]{0:T(1024)S(1)} %get-tuple-element.103, f32[768]{0:T(1024)S(1)} %get-tuple-element.104, f32[768]{0:T(1024)S(1)} %get-tuple-element.57, f32[768]{0:T(1024)S(1)} %get-tuple-element.58, f32[768]{0:T(1024)S(1)} %get-tuple-element.59, f32[768]{0:T(1024)S(1)} %get-tuple-element.60, ...), kind=kLoop, calls=%fused_computation.196 | loop fusion | flops 116391936 | bytes 78796800 | tf_op jit(solution)/shard_map/convert_element_type | solution.py:46
  56.9 1.6 convert_reduce_fusion.1
  58.4 1.0 fusion.146
  60.2 31.5 %psum.64 = f32[256]{0:T(256)S(1)} all-reduce(f32[256]{0:T(256)S(1)} %get-tuple-element.113), channel_id=1, replica_groups=mesh['dp'=8,'sy'=4,'sx'=4] {'sy','sx'}, use_global_device_ids=true, to_apply=%region_2.3 | all-reduce | flops 256 | bytes 2048 | tf_op jit(solution)/shard_map/psum | solution.py:60
  91.8 54.9 %all-reduce.7.cloned.1.call-done = f32[256,256]{1,0:T(8,128)} async-done(((f32[256,256]{1,0:T(8,128)}), f32[256,256]{1,0:T(8,128)}) %all-reduce.7.cloned.1.call-update) | async-done | bytes 262160 | tf_op jit(solution)/shard_map/psum | solution.py:60
  146.7 1.0 multiply_subtract_fusion
  147.9 0.6 select_reduce_fusion
  150.4 0.6 fusion.119
  151.0 0.6 fusion.148
  152.1 0.6 fusion.118
  152.7 0.6 fusion.150
  153.7 0.6 fusion.117
  154.7 0.6 fusion.152
  155.3 0.6 fusion.116
  155.9 1.1 broadcast_multiply_fusion.1
  157.1 4.2 fusion.139
  161.2 1.4 fusion.99
  163.0 0.8 fusion.115
  163.8 0.6 fusion.154
  165.2 0.6 convolution_add_fusion.12
  166.2 0.6 fusion.114
  166.8 0.6 convolution_add_fusion.9
  167.8 0.4 fusion.158
  168.3 0.6 convolution_add_fusion.10
  168.9 1.1 fusion.156
  169.9 0.6 fusion.112
  170.6 0.6 convolution_add_fusion.6
  171.2 1.1 fusion.163
  172.3 1.1 fusion.161
  173.4 1.7 fusion.130
  175.1 1.6 convolution_add_fusion.7
  177.1 1.6 fusion.110
  178.7 0.6 convolution_add_fusion.4
  179.3 0.6 convolution_add_fusion.3
  180.6 0.6 fusion.108
  181.3 0.9 multiply_reduce_fusion
  184.1 2.0 convert_reduce_fusion
  186.2 1.5 fusion.165
  188.2 7.5 %fusion.37 = (f32[768]{0:T(1024)S(1)}, f32[768]{0:T(1024)S(1)}, f32[768]{0:T(1024)S(1)}, f32[768]{0:T(1024)S(1)}, f32[768]{0:T(1024)S(1)}, /*index=5*/f32[768]{0...) fusion(bf16[22,70,768]{2,1,0:T(8,128)(2,1)S(1)} %copy-done.2, ...), kind=kOutput, calls=%fused_computation.135 | convolution fusion | flops 434886912 | bytes 24550400 | tf_op jit(solution)/shard_map/dot_general | solution.py:87
  195.7 7.6 %fusion.97 = (f32[768]{0:T(1024)S(1)}, f32[768]{0:T(1024)S(1)}, f32[768]{0:T(1024)S(1)}, f32[768]{0:T(1024)S(1)}, f32[768]{0:T(1024)S(1)}, /*index=5*/f32[768]{0...) fusion(bf16[22,70,768]{2,1,0:T(8,128)(2,1)S(1)} %copy-done.2, ...), kind=kLoop, calls=%fused_computation.195 | loop fusion | flops 42453504 | bytes 31512576 | tf_op jit(solution)/shard_map/reduce_sum | solution.py:97
  203.3 7.8 %fusion.79 = (f32[768]{0:T(1024)S(1)}, f32[768]{0:T(1024)S(1)}, f32[768]{0:T(1024)S(1)}, f32[768]{0:T(1024)S(1)}, f32[768]{0:T(1024)S(1)}, /*index=5*/f32[768]{0...) fusion(bf16[22,70,768]{2,1,0:T(8,128)(2,1)S(1)} %copy-done.2, ...), kind=kLoop, calls=%fused_computation.177 | loop fusion | flops 42453504 | bytes 31512576 | tf_op jit(solution)/shard_map/reduce_sum | solution.py:97
  212.1 0.7 copy-done.13
  212.9 1.8 broadcast_multiply_fusion
  216.0 14.7 %all-reduce.2 = (f32[]{:T(128)}, f32[10]{0:T(128)}) all-reduce(f32[]{:T(128)S(6)} %sub.41, f32[10]{0:T(128)S(1)} %get-tuple-element.121), channel_id=1, replica_groups=mesh['dp'=8,'sy'=4,'sx'=4] {'dp'}, use_global_device_ids=true, to_apply=%region_6.7 | all-reduce | flops 11 | bytes 88 | tf_op jit(solution)/shard_map/psum | solution.py:74
  230.6 2.1 reduce_sum.569
  233.4 63.9 %all-reduce = (f32[768]{0:T(1024)}, f32[256]{0:T(256)}) all-reduce(f32[768]{0:T(1024)S(1)} %reduce_sum.569, f32[256]{0:T(256)S(1)} %get-tuple-element.126), channel_id=1, replica_groups=mesh['dp'=8,'sy'=4,'sx'=4] {'dp','sy','sx'}, use_global_device_ids=true, to_apply=%region_60.61 | all-reduce | flops 1024 | bytes 8192 | tf_op jit(solution)/shard_map/psum | solution.py:102
  297.3 63.2 %all-reduce.11.cloned.1.call-done = (f32[7,7,768]{2,1,0:T(8,128)}, f32[768,256]{1,0:T(8,128)}) async-done(((f32[7,7,768]{2,1,0:T(8,128)}, f32[768,256]{1,0:T(8,128)}), (f32[7,7,768]{2,1,0:T(8,128)}, f32[768,256]{1,0:T(8,128)})) %all-reduce.11.cloned.1.call-update) | async-done | bytes 936976 | tf_op jit(solution)/shard_map/psum | solution.py:102
  360.6 66.8 %all-reduce.9.cloned.1.call-done = f32[10,256,256]{2,1,0:T(8,128)} async-done(((f32[10,256,256]{2,1,0:T(8,128)}), f32[10,256,256]{2,1,0:T(8,128)}) %all-reduce.9.cloned.1.call-update) | async-done | bytes 2621456 | tf_op jit(solution)/shard_map/psum | solution.py:74
  427.3 1.6 copy.81
  428.9 2.1 copy.82
  431.0 3.4 copy.83
  (129 shorter events, 7.6 us)
Async XLA Ops:
  7.2 149.9 %copy-start = (bf16[10,256,256]{2,1,0:T(8,128)(2,1)S(1)}, bf16[10,256,256]{2,1,0:T(8,128)(2,1)}, u32[]{:S(2)}) copy-start(bf16[10,256,256]{2,1,0:T(8,128)(2,1)} %param.13) | copy-start | bytes 3932164
  7.2 139.5 %all-reduce.7.cloned.1.call-start = ((), (), s32[]{:S(2)}) async-start(), calls=%async_computation | async-start | bytes 524288 | tf_op jit(solution)/shard_map/psum | solution.py:60
  8.4 10.0 %collective-permute-start = (bf16[1,3,64,768]{3,2,1,0:T(8,128)(2,1)S(1)}, bf16[1,3,64,768]{3,2,1,0:T(8,128)(2,1)S(1)}, u32[]{:S(2)}, u32[]{:S(2)}) collective-permute-start(bf16[1,3,64,768]{3,2,1,0:T(8,128)(2,1)S(1)} %get-tuple-element.118), channel_id=1, source_target_pairs={{0,4},{4,8},{8,12},{1,5},{5,9},{9,13},{2,6},{6,10},{10,14},{3,7},{... | collective-permute-start | bytes 884744 | tf_op jit(solution)/shard_map/ppermute | solution.py:20
  12.8 9.8 %collective-permute-start.1 = (bf16[1,3,64,768]{3,2,1,0:T(8,128)(2,1)S(1)}, bf16[1,3,64,768]{3,2,1,0:T(8,128)(2,1)S(1)}, u32[]{:S(2)}, u32[]{:S(2)}) collective-permute-start(bf16[1,3,64,768]{3,2,1,0:T(8,128)(2,1)S(1)} %get-tuple-element.117), channel_id=1, source_target_pairs={{4,0},{8,4},{12,8},{5,1},{9,5},{13,9},{6,2},{10,6},{14,10},{7,3},{... | collective-permute-start | bytes 884744 | tf_op jit(solution)/shard_map/ppermute | solution.py:23
  20.0 13.2 %copy-start.14 = (f32[768]{0:T(1024)S(1)}, f32[768]{0:T(1024)}, u32[]{:S(2)}) copy-start(f32[768]{0:T(1024)} %param.10) | copy-start | bytes 9220
  22.8 5.6 %collective-permute-start.2 = (bf16[1,22,3,768]{3,2,1,0:T(4,128)(2,1)S(1)}, bf16[1,22,3,768]{3,2,1,0:T(4,128)(2,1)S(1)}, u32[]{:S(2)}, u32[]{:S(2)}) collective-permute-start(bf16[1,22,3,768]{3,2,1,0:T(4,128)(2,1)S(1)} %get-tuple-element.115), channel_id=1, source_target_pairs={{0,1},{1,2},{2,3},{4,5},{5,6},{6,7},{8,9},{9,10},{10,11},{12,13},{... | collective-permute-start | bytes 304136 | tf_op jit(solution)/shard_map/ppermute | solution.py:20
  26.0 5.8 %collective-permute-start.3 = (bf16[1,22,3,768]{3,2,1,0:T(4,128)(2,1)S(1)}, bf16[1,22,3,768]{3,2,1,0:T(4,128)(2,1)S(1)}, u32[]{:S(2)}, u32[]{:S(2)}) collective-permute-start(bf16[1,22,3,768]{3,2,1,0:T(4,128)(2,1)S(1)} %get-tuple-element.116), channel_id=1, source_target_pairs={{1,0},{2,1},{3,2},{5,4},{6,5},{7,6},{9,8},{10,9},{11,10},{13,12},{... | collective-permute-start | bytes 304136 | tf_op jit(solution)/shard_map/ppermute | solution.py:23
  33.2 23.6 %copy-start.1 = (bf16[22,70,768]{2,1,0:T(8,128)(2,1)}, bf16[22,70,768]{2,1,0:T(8,128)(2,1)S(1)}, u32[]{:S(2)}) copy-start(bf16[22,70,768]{2,1,0:T(8,128)(2,1)S(1)} %maximum_bitcast_fusion) | copy-start | bytes 7096324
  33.2 23.6 %copy-start.15 = (bf16[768,256]{1,0:T(8,128)(2,1)S(1)}, bf16[768,256]{1,0:T(8,128)(2,1)}, u32[]{:S(2)}) copy-start(bf16[768,256]{1,0:T(8,128)(2,1)} %param.11) | copy-start | bytes 1179652
  33.2 23.6 %copy-start.17 = (f32[256]{0:T(256)S(1)}, f32[256]{0:T(256)}, u32[]{:S(2)}) copy-start(f32[256]{0:T(256)} %param.12) | copy-start | bytes 3076
  56.8 1.6 copy-start.4
  59.5 301.0 %all-reduce.11.cloned.1.call-start = ((), (), s32[]{:S(2)}) async-start(), calls=%async_computation.2 | async-start | bytes 1916928 | tf_op jit(solution)/shard_map/psum | solution.py:102
  147.7 5.0 %copy-start.10 = (f32[256,256]{1,0:T(8,128)}, f32[256,256]{1,0:T(8,128)S(1)}, u32[]{:S(2)}) copy-start(f32[256,256]{1,0:T(8,128)S(1)} %multiply_subtract_fusion) | copy-start | bytes 786436
  149.6 4.7 %copy-start.6 = (f32[256,256]{0,1:T(8,128)}, f32[256,256]{0,1:T(8,128)S(1)}, u32[]{:S(2)}) copy-start(f32[256,256]{0,1:T(8,128)S(1)} %fusion.120) | copy-start | bytes 786436
  152.1 5.0 %copy-start.18 = (f32[10]{0:T(128)S(1)}, f32[10]{0:T(128)}, u32[]{:S(2)}) copy-start(f32[10]{0:T(128)} %param.14) | copy-start | bytes 124
  157.1 4.2 copy-start.8
  173.4 5.8 %copy-start.12 = (f32[256,256]{1,0:T(8,128)S(1)}, f32[256,256]{1,0:T(8,128)}, u32[]{:S(2)}) copy-start(f32[256,256]{1,0:T(8,128)} %fusion.163) | copy-start | bytes 786436
  173.4 6.8 %copy-start.7 = (f32[256,256]{0,1:T(8,128)S(1)}, f32[256,256]{0,1:T(8,128)}, u32[]{:S(2)}) copy-start(f32[256,256]{0,1:T(8,128)} %copy-done.6) | copy-start | bytes 786436
  175.1 5.5 %copy-start.11 = (f32[256,256]{1,0:T(8,128)S(1)}, f32[256,256]{1,0:T(8,128)}, u32[]{:S(2)}) copy-start(f32[256,256]{1,0:T(8,128)} %copy-done.10) | copy-start | bytes 786436
  184.1 2.1 copy-start.5
  186.1 1.9 copy-start.2
  186.2 2.0 copy-start.16
  195.6 7.6 %copy-start.3 = (f32[1024,768]{1,0:T(8,128)}, f32[1024,768]{1,0:T(8,128)S(1)}, u32[]{:S(2)}) copy-start(f32[1024,768]{1,0:T(8,128)S(1)} %get-tuple-element.125) | copy-start | bytes 9437188
  203.3 9.6 %copy-start.9 = (f32[256,256]{1,0:T(8,128)S(1)}, f32[256,256]{1,0:T(8,128)}, u32[]{:S(2)}) copy-start(f32[256,256]{1,0:T(8,128)} %copy-done.8) | copy-start | bytes 786436
  212.1 0.7 copy-start.13
  212.8 214.5 %all-reduce.9.cloned.1.call-start = ((), (), s32[]{:S(2)}) async-start(), calls=%async_computation.1 | async-start | bytes 5242880 | tf_op jit(solution)/shard_map/psum | solution.py:74
Sparse Core Ops, SparseCore 0:
  59.6 86.9 all-reduce.6
  212.9 147.5 all-reduce.10
  363.5 63.7 all-reduce.8
where the time goes:
time: 449 us; the launch traced here: 442 us
  waiting for transfers between devices  192 us (43%)
  blocking collectives  110 us (24%)
  other arithmetic  48 us (11%)
  matrix products  44.6 us (10%)
  between operations  20.9 us (5%)
  local copies, waits for them, and re-layouts  15.9 us (4%)
  starting transfers between devices  10.3 us (2%)
    psum x1, waiting for transfers between devices, body(): lax.psum((loss_part, class_local, logit_grad), 'dp')  66.8 us
    psum x1, blocking collectives, body(): lax.psum((weight_grad, depth_grad, depth_bias_grad, bias_grad), ('dp', 's...  63.9 us
    psum x1, waiting for transfers between devices, body(): lax.psum((weight_grad, depth_grad, depth_bias_grad, bias_grad), ('dp', 's...  63.2 us
    psum x1, waiting for transfers between devices, body(): gram, colsum = lax.psum((gram, colsum), ('sy', 'sx'))  54.9 us
    psum x1, blocking collectives, body(): gram, colsum = lax.psum((gram, colsum), ('sy', 'sx'))  31.5 us
    convert_element_type x1, other arithmetic, taps_conv(): return total.astype(jnp.bfloat16)  23.6 us
    reduce_sum x2, other arithmetic, body(): jnp.sum(window.astype(jnp.float32) * conv_grad.astype(jnp.float32), axis=...  15.4 us
    psum x1, blocking collectives, body(): lax.psum((loss_part, class_local, logit_grad), 'dp')  14.7 us
  transfers between devices with their start and end apart: 7, of which 6 were waited for; matrix products, arithmetic and copies ran while one was open for 2% of the time, Pallas kernels for 0%

commit v1 on v0

v1 whole, which is shorter than its diff:
```python
import functools

import jax
import jax.numpy as jnp
from jax import lax
from jax.experimental import pallas as pl
from jax.experimental.pallas import tpu as pltpu
from jax.sharding import PartitionSpec as P

MESH = pl.DeviceIdType.MESH
KERNEL = 7
NEWTON_STEPS = 5
ROWS = 16
COLS = 64
TILES = 6
CHANNELS = 768
REDUCED = 256
CLASSES = 10
PITCH = 80
BLOCK0 = 8
epsilon = 1e-05
loss_scale = 64.0
f32 = jnp.float32
bf16 = jnp.bfloat16


def lanes_of(tile):
    return pl.ds(pl.multiple_of(tile * 128, 128), 128)


def split(value):
    high = value.astype(bf16)
    return high, (value - high.astype(f32)).astype(bf16)


def products(*pairs):
    left, right = [], []
    for (a_high, a_low), (b_high, b_low) in pairs:
        left += [a_low, a_high, a_high]
        right += [b_high, b_low, b_high]
    return jnp.dot(
        jnp.concatenate(left, axis=1), jnp.concatenate(right, axis=0), preferred_element_type=f32
    )


def main_kernel(
    x_ref, w_ref, db_ref, rw_ref, rb_ref, cw_ref, cb_ref, lab_ref,
    wg_out, dg_out, root_out, small_out,
    image, conv32, conv, before, feat, pre, cgrad,
    csend, ksend, hrow, hcol, hcor,
    gram, grecv, gfull, colsum, crecv,
    ys, zs, ts, sym, mean_term,
    wsend, wrecv, wx, depth, dsend, drecv, dx,
    halo_send, halo_recv, g_send, g_recv, c_send, c_recv, a_send, a_recv,
    x_send, x_recv, s_send, s_recv, w_send, w_recv, wx_send, wx_recv, wa_send, wa_recv,
    d_send, d_recv, dx_send, dx_recv, da_send, da_recv,
):
    idp, iz, iy = lax.axis_index("dp"), lax.axis_index("sy"), lax.axis_index("sx")
    images = 8
    count = ROWS * COLS * 16
    me = iz * 4 + iy

    def plane(offset, sign=1):
        dz, dy = divmod(offset, 4)
        pz, py = lax.rem(iz + 4 + sign * dz, 4), lax.rem(iy + 4 + sign * dy, 4)
        return (idp, pz, py), pz * 4 + py

    def line(offset, sign=1):
        other = lax.rem(idp + 8 + sign * offset, 8)
        return (other, iz, iy), other

    def send(src, dst, send_sem, recv_sem, device):
        copy = pltpu.make_async_remote_copy(
            src_ref=src, dst_ref=dst, send_sem=send_sem, recv_sem=recv_sem,
            device_id=device, device_id_type=MESH,
        )
        return copy

    barrier = pltpu.get_barrier_semaphore()
    for offset in range(1, 16):
        pl.semaphore_signal(barrier, inc=1, device_id=plane(offset)[0], device_id_type=MESH)
    for offset in range(1, 8):
        pl.semaphore_signal(barrier, inc=1, device_id=line(offset)[0], device_id_type=MESH)

    def fill(tile, carry):
        lanes = lanes_of(tile)
        for row in range(ROWS):
            start = (row + 3) * PITCH + BLOCK0
            image[tile, start : start + COLS, :] = x_ref[0, row, :, lanes].astype(f32)
        for side in range(2):
            for col in range(3):
                at = BLOCK0 + col + (0 if side == 0 else COLS - 3)
                strip = image[tile, pl.ds(3 * PITCH + at, ROWS, stride=PITCH), :]
                csend[side, col, :, lanes] = strip.astype(bf16)
                for end in range(2):
                    ksend[end * 2 + side, col, :, lanes] = strip[8 * end : 8 * end + 8].astype(bf16)
        return carry

    lax.fori_loop(0, TILES, fill, 0)
    pl.semaphore_wait(barrier, 22)

    up, down = lax.rem(iz + 3, 4), lax.rem(iz + 1, 4)
    left, right = lax.rem(iy + 3, 4), lax.rem(iy + 1, 4)
    halo = [
        (x_ref.at[0, pl.ds(ROWS - 3, 3)], hrow.at[0], (idp, down, iy)),
        (x_ref.at[0, pl.ds(0, 3)], hrow.at[1], (idp, up, iy)),
        (csend.at[1], hcol.at[0], (idp, iz, right)),
        (csend.at[0], hcol.at[1], (idp, iz, left)),
        (ksend.at[3], hcor.at[0], (idp, down, right)),
        (ksend.at[2], hcor.at[1], (idp, down, left)),
        (ksend.at[1], hcor.at[2], (idp, up, right)),
        (ksend.at[0], hcor.at[3], (idp, up, left)),
    ]
    copies = [
        send(src, dst, halo_send.at[i], halo_recv.at[i], device)
        for i, (src, dst, device) in enumerate(halo)
    ]
    for copy in copies:
        copy.start()
    for copy in copies:
        copy.wait()
    has_up, has_down, has_left, has_right = iz > 0, iz < 3, iy > 0, iy < 3

    def edges(tile, carry):
        lanes = lanes_of(tile)
        for end in range(2):
            has_row = (has_up, has_down)[end]
            for row in range(3):
                start = (row + 19 * end) * PITCH + BLOCK0
                strip = hrow[end, row, :, lanes].astype(f32)
                image[tile, start : start + COLS, :] = jnp.where(has_row, strip, 0.0)
        for side in range(2):
            has_col = (has_left, has_right)[side]
            for col in range(3):
                at = BLOCK0 - 3 + col + side * (COLS + 3)
                strip = hcol[side, col, :, lanes].astype(f32)
                image[tile, pl.ds(3 * PITCH + at, ROWS, stride=PITCH), :] = jnp.where(
                    has_col, strip, 0.0
                )
                for end in range(2):
                    has_both = jnp.logical_and((has_up, has_down)[end], has_col)
                    strip = hcor[end * 2 + side, col, :, lanes].astype(f32)
                    strip = jnp.where(has_both, strip, 0.0)
                    strip = strip[5:8] if end == 0 else strip[0:3]
                    image[tile, pl.ds(19 * end * PITCH + at, 3, stride=PITCH), :] = strip
        return carry

    lax.fori_loop(0, TILES, edges, 0)

    def conv_tile(tile, carry):
        lanes = lanes_of(tile)

        def group(jg, inner):
            acc = [jnp.broadcast_to(db_ref[:, lanes], (8, 128))] * ROWS
            for b in range(KERNEL):
                taps = [jnp.broadcast_to(w_ref[a, pl.ds(b, 1), lanes], (8, 128)) for a in range(KERNEL)]
                for row in range(ROWS + 6):
                    x = image[tile, pl.ds(jg * 8 + (row * PITCH + BLOCK0 - 3 + b), 8), :]
                    for a in range(KERNEL):
                        if 0 <= row - a < ROWS:
                            acc[row - a] = acc[row - a] + x * taps[a]
            for row in range(ROWS):
                conv32[pl.ds(pl.multiple_of(jg * 8 + row * COLS, 8), 8), :] = acc[row]
            return inner

        lax.fori_loop(0, COLS // 8, group, 0)
        conv[:, lanes] = conv32[...].astype(bf16)
        return carry

    lax.fori_loop(0, TILES, conv_tile, 0)

    colsum[...] = jnp.zeros_like(colsum)
    for part in range(4):
        rows = pl.ds(part * 256, 256)
        value = jnp.dot(conv[rows, :], rw_ref[...], preferred_element_type=f32) + rb_ref[...]
        before[rows, :] = value
        active = (value / (1.0 + jnp.exp(-value))).astype(bf16)
        feat[rows, :] = active
        colsum[...] += jnp.sum(active.astype(f32), axis=0, keepdims=True)
    total = lax.dot_general(
        feat[...], feat[...], (((0,), (0,)), ((), ())), preferred_element_type=f32
    )
    gram[...] = total.reshape(16, 16, REDUCED)
    crecv[me] = colsum[...]

    copies = []
    for offset in range(1, 16):
        device, index = plane(offset)
        copies.append(send(gram.at[index], grecv.at[offset], g_send.at[offset], g_recv.at[offset], device))
        copies.append(send(colsum, crecv.at[me], c_send.at[offset], c_recv.at[offset], device))
    for copy in copies:
        copy.start()
    for offset in range(1, 16):
        _, source = plane(offset, -1)
        send(gram.at[0], grecv.at[offset], g_send.at[offset], g_recv.at[offset], plane(offset)[0]).wait_recv()
        send(colsum, crecv.at[source], c_send.at[offset], c_recv.at[offset], plane(offset)[0]).wait_recv()
    mine = gram[me]
    for offset in range(1, 16):
        mine = mine + grecv[offset]
    gfull[me] = mine
    gathers = []
    for offset in range(1, 16):
        device, _ = plane(offset)
        gathers.append(send(gfull.at[me], gfull.at[me], a_send.at[offset], a_recv.at[offset], device))
    for copy in gathers:
        copy.start()
    for copy in copies:
        copy.wait_send()
    for offset in range(1, 16):
        _, source = plane(offset, -1)
        send(gfull.at[source], gfull.at[source], a_send.at[offset], a_recv.at[offset], plane(offset)[0]).wait_recv()
    for copy in gathers:
        copy.wait_send()

    mean = crecv[0]
    for index in range(1, 16):
        mean = mean + crecv[index]
    mean = mean * (1.0 / count)
    wide = jnp.broadcast_to(mean, (REDUCED, REDUCED))
    sigma = gfull[...].reshape(REDUCED, REDUCED) * (1.0 / count) - wide.T * wide
    row_id = lax.broadcasted_iota(jnp.int32, (REDUCED, REDUCED), 0)
    col_id = lax.broadcasted_iota(jnp.int32, (REDUCED, REDUCED), 1)
    diagonal = row_id == col_id
    identity15 = jnp.where(diagonal, 1.5, 0.0)
    trace = jnp.sum(
        jnp.sum(jnp.where(diagonal, sigma, 0.0), axis=0, keepdims=True), axis=1, keepdims=True
    ) + epsilon
    start = sigma / trace

    def keep(ref, step, value):
        high, low = split(value)
        ref[step, 0] = high
        ref[step, 1] = low

    def kept(ref, step):
        return ref[step, 0], ref[step, 1]

    keep(ys, 0, start)
    keep(ts, 0, identity15 - 0.5 * start)
    keep(ys, 1, products((kept(ys, 0), kept(ts, 0))))
    for step in range(1, NEWTON_STEPS):
        inverse = kept(ts, 0) if step == 1 else kept(zs, step)
        factor = identity15 - 0.5 * products((inverse, kept(ys, step)))
        keep(ts, step, factor)
        if step < NEWTON_STEPS - 1:
            keep(zs, step + 1, products((kept(ts, step), inverse)))
            keep(ys, step + 1, products((kept(ys, step), kept(ts, step))))
    last = products((kept(ys, NEWTON_STEPS - 1), kept(ts, NEWTON_STEPS - 1)))
    root_scale = jnp.sqrt(trace)
    root = root_scale * last
    root_out[idp] = root.astype(bf16)

    class_id = lax.broadcasted_iota(jnp.int32, (1, CLASSES), 1)
    logits = cb_ref[...]
    for k in range(CLASSES):
        weighted = jnp.sum(cw_ref[k].astype(f32) * root, axis=0, keepdims=True)
        logits = logits + jnp.where(class_id == k, jnp.sum(weighted, axis=1, keepdims=True), 0.0)
    onehot = jnp.where(class_id == lab_ref[0], 1.0, 0.0)
    softplus = jnp.maximum(logits, 0.0) + jnp.log(1.0 + jnp.exp(-jnp.abs(logits)))
    loss = jnp.sum(softplus - onehot * logits, axis=1, keepdims=True)
    logit_grad = (loss_scale / images) * (1.0 / (1.0 + jnp.exp(-logits)) - onehot)
    small_out[idp] = jnp.zeros((8, 128), f32)
    small_out[idp, 0:1, 0:CLASSES] = logit_grad
    small_out[idp, 1:2, :] = jnp.broadcast_to(loss, (1, 128))
    roots, smalls = [], []
    for offset in range(1, 8):
        device, _ = line(offset)
        roots.append(send(root_out.at[idp], root_out.at[idp], x_send.at[offset], x_recv.at[offset], device))
        smalls.append(send(small_out.at[idp], small_out.at[idp], s_send.at[offset], s_recv.at[offset], device))
    for copy in smalls + roots:
        copy.start()

    root_grad = jnp.zeros((REDUCED, REDUCED), f32)
    for k in range(CLASSES):
        root_grad = root_grad + logit_grad[:, k : k + 1] * cw_ref[k].astype(f32)
    root_grad = 0.5 * (root_grad + root_grad.T)
    trace_grad = jnp.sum(jnp.sum(root_grad * last, axis=0, keepdims=True), axis=1, keepdims=True)
    trace_grad = trace_grad * 0.5 / root_scale
    seed = root_scale * root_grad
    d_y = split(seed)
    d_t = split(-0.5 * seed)
    d_z = d_t
    d_y = split(products((d_y, kept(ts, 0)), (kept(ys, 0), d_t)))
    for step in range(1, NEWTON_STEPS):
        inverse = kept(ts, 0) if step == 1 else kept(zs, step)
        d_t = split(-0.5 * products((d_z, kept(ys, step)), (inverse, d_y)))
        if step < NEWTON_STEPS - 1:
            d_z = split(products((d_t, inverse), (kept(ts, step), d_z)))
            d_y = split(products((d_y, kept(ts, step)), (kept(ys, step), d_t)))
    start_grad = products((d_y, kept(ts, NEWTON_STEPS - 1)), (kept(ys, NEWTON_STEPS - 1), d_t))
    start_grad = 0.5 * (start_grad + start_grad.T)
    start_value = ys[0, 0].astype(f32) + ys[0, 1].astype(f32)
    inner = jnp.sum(jnp.sum(start_grad * start_value, axis=0, keepdims=True), axis=1, keepdims=True)
    trace_grad = trace_grad - inner / trace
    sigma_grad = start_grad / trace + jnp.where(diagonal, trace_grad, 0.0)
    symmetric = (sigma_grad * (2.0 / count)).astype(bf16)
    sym[...] = symmetric
    mean_high, mean_low = split(jnp.broadcast_to(mean, (8, REDUCED)))
    mean_term[...] = jnp.dot(mean_high, symmetric, preferred_element_type=f32) + jnp.dot(
        mean_low, symmetric, preferred_element_type=f32
    )

    depth[...] = jnp.zeros_like(depth)
    bias_grad = jnp.zeros((1, REDUCED), f32)
    for part in range(4):
        rows = pl.ds(part * 256, 256)
        feat_grad = jnp.dot(feat[rows, :], sym[...], preferred_element_type=f32) - mean_term[0:1, :]
        value = before[rows, :]
        gate = 1.0 / (1.0 + jnp.exp(-value))
        pre_grad = (feat_grad * gate * (1.0 + value * (1.0 - gate))).astype(bf16)
        pre[rows, :] = pre_grad
        bias_grad = bias_grad + jnp.sum(pre_grad.astype(f32), axis=0, keepdims=True)
        conv_grad = lax.dot_general(
            pre_grad, rw_ref[...], (((1,), (1,)), ((), ())), preferred_element_type=f32
        ).astype(bf16).astype(f32)
        for tile in range(TILES):
            cgrad[tile, rows, :] = conv_grad[:, tile * 128 : tile * 128 + 128]
    weight_grad = lax.dot_general(
        conv[...], pre[...], (((0,), (0,)), ((), ())), preferred_element_type=f32
    )
    wsend[...] = weight_grad.astype(bf16).reshape(16, 48, REDUCED)
    depth[0, 15:16, :] = bias_grad[:, 0:128]
    depth[1, 15:16, :] = bias_grad[:, 128:256]

    w_copies = []
    for offset in range(1, 16):
        device, index = plane(offset)
        w_copies.append(send(wsend.at[index], wrecv.at[offset], w_send.at[offset], w_recv.at[offset], device))
    for copy in w_copies:
        copy.start()

    def depth_tile(tile, carry):
        for b in range(KERNEL):

            def group(jg, acc):
                acc = list(acc)
                grads = [
                    cgrad[tile, pl.ds(pl.multiple_of(jg * 8 + row * COLS, 8), 8), :]
                    for row in range(ROWS)
                ]
                for row in range(ROWS + 6):
                    x = image[tile, pl.ds(jg * 8 + (row * PITCH + BLOCK0 - 3 + b), 8), :]
                    for a in range(KERNEL):
                        if 0 <= row - a < ROWS:
                            acc[a] = acc[a] + x * grads[row - a]
                if b == 0:
                    partial = grads[0]
                    for row in range(1, ROWS):
                        partial = partial + grads[row]
                    acc[KERNEL] = acc[KERNEL] + partial
                return tuple(acc)

            zero = jnp.zeros((8, 128), f32)
            sums = lax.fori_loop(0, COLS // 8, group, (zero,) * (KERNEL + (b == 0)))
            for a in range(KERNEL):
                depth[tile, a * 8 + b : a * 8 + b + 1, :] = jnp.sum(sums[a], axis=0, keepdims=True)
            if b == 0:
                depth[tile, 7:8, :] = jnp.sum(sums[KERNEL], axis=0, keepdims=True)
        return carry

    lax.fori_loop(0, 3, depth_tile, 0)

    for copy in w_copies:
        copy.wait()
    w_sum = wsend[me].astype(f32)
    for offset in range(1, 16):
        w_sum = w_sum + wrecv[offset].astype(f32)
    wx[idp] = w_sum.astype(bf16)
    wx_copies = []
    for offset in range(1, 8):
        device, _ = line(offset)
        wx_copies.append(send(wx.at[idp], wx.at[idp], wx_send.at[offset], wx_recv.at[offset], device))
    for copy in wx_copies:
        copy.start()
    lax.fori_loop(3, 5, depth_tile, 0)
    for offset in range(1, 8):
        _, source = line(offset, -1)
        send(wx.at[source], wx.at[source], wx_send.at[offset], wx_recv.at[offset], line(offset)[0]).wait_recv()
    for copy in wx_copies:
        copy.wait_send()
    w_sum = wx[0].astype(f32)
    for index in range(1, 8):
        w_sum = w_sum + wx[index].astype(f32)
    wg_out[me] = w_sum.astype(bf16)
    wa_copies = []
    for offset in range(1, 16):
        device, _ = plane(offset)
        wa_copies.append(send(wg_out.at[me], wg_out.at[me], wa_send.at[offset], wa_recv.at[offset], device))
    for copy in wa_copies:
        copy.start()
    lax.fori_loop(5, 6, depth_tile, 0)

    for group8 in range(8):
        for half in range(2):
            for third in range(3):
                dsend[group8 * 2 + half, :, third * 128 : third * 128 + 128] = depth[
                    half * 3 + third, group8 * 8 : group8 * 8 + 8, :
                ].astype(bf16)
    d_copies = []
    for offset in range(1, 16):
        device, index = plane(offset)
        d_copies.append(send(dsend.at[index], drecv.at[offset], d_send.at[offset], d_recv.at[offset], device))
    for copy in d_copies:
        copy.start()
    for copy in d_copies:
        copy.wait()
    d_sum = dsend[me].astype(f32)
    for offset in range(1, 16):
        d_sum = d_sum + drecv[offset].astype(f32)
    dx[idp] = d_sum.astype(bf16)
    dx_copies = []
    for offset in range(1, 8):
        device, _ = line(offset)
        dx_copies.append(send(dx.at[idp], dx.at[idp], dx_send.at[offset], dx_recv.at[offset], device))
    for copy in dx_copies:
        copy.start()
    for offset in range(1, 8):
        _, source = line(offset, -1)
        send(dx.at[source], dx.at[source], dx_send.at[offset], dx_recv.at[offset], line(offset)[0]).wait_recv()
    for copy in dx_copies:
        copy.wait_send()
    d_sum = dx[0].astype(f32)
    for index in range(1, 8):
        d_sum = d_sum + dx[index].astype(f32)
    dg_out[me] = d_sum.astype(bf16)
    da_copies = []
    for offset in range(1, 16):
        device, _ = plane(offset)
        da_copies.append(send(dg_out.at[me], dg_out.at[me], da_send.at[offset], da_recv.at[offset], device))
    for copy in da_copies:
        copy.start()
    for offset in range(1, 16):
        _, source = plane(offset, -1)
        device = plane(offset)[0]
        send(wg_out.at[source], wg_out.at[source], wa_send.at[offset], wa_recv.at[offset], device).wait_recv()
        send(dg_out.at[source], dg_out.at[source], da_send.at[offset], da_recv.at[offset], device).wait_recv()
    for offset in range(1, 8):
        _, source = line(offset, -1)
        device = line(offset)[0]
        send(root_out.at[source], root_out.at[source], x_send.at[offset], x_recv.at[offset], device).wait_recv()
        send(small_out.at[source], small_out.at[source], s_send.at[offset], s_recv.at[offset], device).wait_recv()
    for copy in wa_copies + da_copies + roots + smalls:
        copy.wait_send()


def finish_kernel(wg, dg, roots, smalls, loss, depth_grad, depth_bias, weight, bias, class_weight, class_bias):
    k = pl.program_id(0)
    lane = lax.broadcasted_iota(jnp.int32, (1, 128), 1)
    total = jnp.zeros((REDUCED, REDUCED), f32)
    for image in range(8):
        factor = jnp.sum(jnp.where(lane == k, smalls[image, 0:1, :], 0.0), axis=1, keepdims=True)
        total = total + factor * roots[image].astype(f32)
    class_weight[0] = total

    @pl.when(k == 0)
    def _():
        weight[...] = wg[...].astype(f32).reshape(CHANNELS, REDUCED)
        for half in range(2):
            lanes = slice(half * 384, half * 384 + 384)
            for a in range(KERNEL):
                depth_grad[a, :, lanes] = dg[a * 2 + half, 0:7, :].astype(f32)
            depth_bias[:, lanes] = dg[half, 7:8, :].astype(f32)
        bias[:, 0:128] = dg[2, 7:8, 0:128].astype(f32)
        bias[:, 128:256] = dg[2, 7:8, 128:256].astype(f32)
        small = smalls[0]
        for image in range(1, 8):
            small = small + smalls[image]
        class_bias[...] = small[0:1, 0:CLASSES]
        loss[...] = small[1:2, 0:1] * (1.0 / 8)


def body(
    features, depth_weight, depth_bias, reduce_weight, reduce_bias, class_weight, class_bias, labels
):
    vmem = pl.BlockSpec(memory_space=pltpu.VMEM)
    smem = pl.BlockSpec(memory_space=pltpu.SMEM)
    dma = pltpu.SemaphoreType.DMA
    scratch = [
        pltpu.VMEM((TILES, (ROWS + 6) * PITCH, 128), f32),
        pltpu.VMEM((ROWS * COLS, 128), f32),
        pltpu.VMEM((ROWS * COLS, CHANNELS), bf16),
        pltpu.VMEM((ROWS * COLS, REDUCED), f32),
        pltpu.VMEM((ROWS * COLS, REDUCED), bf16),
        pltpu.VMEM((ROWS * COLS, REDUCED), bf16),
        pltpu.VMEM((TILES, ROWS * COLS, 128), f32),
        pltpu.VMEM((2, 3, 16, CHANNELS), bf16),
        pltpu.VMEM((4, 3, 8, CHANNELS), bf16),
        pltpu.VMEM((2, 3, COLS, CHANNELS), bf16),
        pltpu.VMEM((2, 3, 16, CHANNELS), bf16),
        pltpu.VMEM((4, 3, 8, CHANNELS), bf16),
        pltpu.VMEM((16, 16, REDUCED), f32),
        pltpu.VMEM((16, 16, REDUCED), f32),
        pltpu.VMEM((16, 16, REDUCED), f32),
        pltpu.VMEM((1, REDUCED), f32),
        pltpu.VMEM((16, 1, REDUCED), f32),
        pltpu.VMEM((NEWTON_STEPS, 2, REDUCED, REDUCED), bf16),
        pltpu.VMEM((NEWTON_STEPS, 2, REDUCED, REDUCED), bf16),
        pltpu.VMEM((NEWTON_STEPS, 2, REDUCED, REDUCED), bf16),
        pltpu.VMEM((REDUCED, REDUCED), bf16),
        pltpu.VMEM((8, REDUCED), f32),
        pltpu.VMEM((16, 48, REDUCED), bf16),
        pltpu.VMEM((16, 48, REDUCED), bf16),
        pltpu.VMEM((8, 48, REDUCED), bf16),
        pltpu.VMEM((TILES, 64, 128), f32),
        pltpu.VMEM((16, 8, 384), bf16),
        pltpu.VMEM((16, 8, 384), bf16),
        pltpu.VMEM((8, 8, 384), bf16),
        dma((8,)), dma((8,)),
        dma((16,)), dma((16,)), dma((16,)), dma((16,)), dma((16,)), dma((16,)),
        dma((8,)), dma((8,)), dma((8,)), dma((8,)),
        dma((16,)), dma((16,)), dma((8,)), dma((8,)), dma((16,)), dma((16,)),
        dma((16,)), dma((16,)), dma((8,)), dma((8,)), dma((16,)), dma((16,)),
    ]
    wg, dg, roots, smalls = pl.pallas_call(
        main_kernel,
        out_shape=(
            jax.ShapeDtypeStruct((16, 48, REDUCED), bf16),
            jax.ShapeDtypeStruct((16, 8, 384), bf16),
            jax.ShapeDtypeStruct((8, REDUCED, REDUCED), bf16),
            jax.ShapeDtypeStruct((8, 8, 128), f32),
        ),
        in_specs=[vmem] * 7 + [smem],
        out_specs=(vmem,) * 4,
        scratch_shapes=scratch,
        compiler_params=pltpu.CompilerParams(
            collective_id=0, has_side_effects=True, vmem_limit_bytes=50 << 20
        ),
        name="pooling_step",
    )(
        features, depth_weight, depth_bias.reshape(1, CHANNELS), reduce_weight,
        reduce_bias.reshape(1, REDUCED), class_weight, class_bias.reshape(1, CLASSES), labels,
    )
    whole = lambda *shape: pl.BlockSpec(shape, lambda k: (0,) * len(shape))
    loss, depth_grad, depth_bias_grad, weight_grad, bias_grad, class_grad, class_bias_grad = pl.pallas_call(
        finish_kernel,
        grid=(CLASSES,),
        out_shape=(
            jax.ShapeDtypeStruct((1, 1), f32),
            jax.ShapeDtypeStruct((KERNEL, KERNEL, CHANNELS), f32),
            jax.ShapeDtypeStruct((1, CHANNELS), f32),
            jax.ShapeDtypeStruct((CHANNELS, REDUCED), f32),
            jax.ShapeDtypeStruct((1, REDUCED), f32),
            jax.ShapeDtypeStruct((CLASSES, REDUCED, REDUCED), f32),
            jax.ShapeDtypeStruct((1, CLASSES), f32),
        ),
        in_specs=[whole(16, 48, REDUCED), whole(16, 8, 384), whole(8, REDUCED, REDUCED), whole(8, 8, 128)],
        out_specs=(
            whole(1, 1), whole(KERNEL, KERNEL, CHANNELS), whole(1, CHANNELS), whole(CHANNELS, REDUCED),
            whole(1, REDUCED), pl.BlockSpec((1, REDUCED, REDUCED), lambda k: (k, 0, 0)), whole(1, CLASSES),
        ),
        compiler_params=pltpu.CompilerParams(vmem_limit_bytes=24 << 20),
        name="outputs",
    )(wg, dg, roots, smalls)
    return (
        loss.reshape(()), depth_grad, depth_bias_grad.reshape(CHANNELS), weight_grad,
        bias_grad.reshape(REDUCED), class_grad, class_bias_grad.reshape(CLASSES),
    )


def solution(mesh):
    placed = (P("dp", "sy", "sx", None), P(), P(), P(), P(), P(), P(), P("dp"))
    return jax.shard_map(
        body,
        mesh=mesh,
        in_specs=placed,
        out_specs=(P(), P(), P(), P(), P(), P(), P()),
        check_vma=False,
    )
```

time: 449 us -> 101 us (0.22); the launches traced: 442 us -> 101 us
  waiting for transfers between devices: 192 us -> 0 us
  blocking collectives: 110 us -> 0 us
  Pallas kernels: 0 us -> 93.6 us
  other arithmetic: 48 us -> 0.6 us
  matrix products: 44.6 us -> 0 us
  between operations: 20.9 us -> 1.29 us
  local copies, waits for them, and re-layouts: 15.9 us -> 5.25 us
  starting transfers between devices: 10.3 us -> 0 us
    psum x3 -> x0, waiting for transfers between devices: 185 us -> none  [the longest x1 66.8 us: body(): lax.psum((loss_part, class_local, logit_grad), 'dp')]
    psum x3 -> x0, blocking collectives: 110 us -> none  [the longest x1 63.9 us: body(): lax.psum((weight_grad, depth_grad, depth_bias_grad, bias_grad), ('dp', 's...]
    pallas_call x0 -> x2, Pallas kernels: none -> 93.6 us  [the longest x1 87.4 us: body(): pl.pallas_call(main_kernel, out_shape=(jax.ShapeDtypeStruct((16, 48, REDU...]
    dot_general x48 -> x0, matrix products: 44.6 us -> none  [the longest x15 9.51 us: matrix_root(): current = jnp.dot(current, factor, precision=highest)]
    convert_element_type x2 -> x0, other arithmetic: 23.8 us -> none  [the longest x1 23.6 us: taps_conv(): return total.astype(jnp.bfloat16)]
    reduce_sum x5 -> x0, other arithmetic: 19.9 us -> none  [the longest x2 15.4 us: body(): jnp.sum(window.astype(jnp.float32) * conv_grad.astype(jnp.float32), axis=...]
    ppermute x4 -> x0, starting transfers between devices: 10.2 us -> none  [the longest x2 7.6 us: with_halo(): lax.ppermute(lax.slice_in_dim(block, block.shape[dim] - width, None, axis...]
    ppermute x4 -> x0, waiting for transfers between devices: 7.53 us -> none  [the longest x2 5.97 us: with_halo(): lax.ppermute(lax.slice_in_dim(block, 0, width, axis=dim), axis, backward)]
  transfers between devices with their start and end apart: 7 -> 0, of which waited for: 6 -> 0; matrix products, arithmetic and copies ran while one was open for 2% -> 0% of each run, Pallas kernels for 0% -> 0%
where the time goes in v1:
time: 101 us
  Pallas kernels  93.6 us (93%)
  local copies, waits for them, and re-layouts  5.25 us (5%)
  between operations  1.29 us (1%)
    pallas_call x1, Pallas kernels, body(): pl.pallas_call(main_kernel, out_shape=(jax.ShapeDtypeStruct((16, 48, REDU...  87.4 us
    pallas_call x1, Pallas kernels, body(): pl.pallas_call(finish_kernel, grid=(CLASSES,), out_shape=(jax.ShapeDtypeS...  6.18 us
    unnamed x10, local copies, waits for them, and re-layouts  4.56 us

profile of v1, /device:TPU:1, one launch (start us, length us, event | category | flops | bytes accessed | tf_op | source)
XLA Modules:
  0.0 100.7 jit_solution(7938659073663204758)
XLA Ops:
  1.3 0.7 reshape.35.db_ref
  2.0 0.0 copy-start
  2.0 1.3 %copy-done = bf16[10,256,256]{2,1,0:T(8,128)(2,1)S(1)} copy-done((bf16[10,256,256]{2,1,0:T(8,128)(2,1)S(1)}, bf16[10,256,256]{2,1,0:T(8,128)(2,1)}, u32[]{:S(2)}) %copy-start) | copy-done | bytes 1310744
  3.3 0.0 copy-start.1
  3.3 1.0 copy-done.1
  4.3 0.0 copy-start.2
  4.3 0.9 copy-done.2
  5.2 0.0 copy-start.3
  5.2 0.7 copy-done.3
  5.9 0.0 copy-start.4
  5.9 0.7 copy-done.4
  6.5 87.4 %pooling_step.1 = (bf16[16,48,256]{2,1,0:T(8,128)(2,1)S(1)}, bf16[16,8,384]{2,1,0:T(8,128)(2,1)S(1)}, bf16[8,256,256]{2,1,0:T(8,128)(2,1)S(1)}, f32[8,8,128]{2,1,0:T(8,128)S(1)}) custom-call(bf16[1,16,64,768]{3,2,1,0:T(8,128)(2,1)} %x_ref.1, f32[7,7,768]{2,1,0:T(8,128)S(1)} %copy-done.2, f32[1,768]{1,0:T(1,128)S(1)} %reshape.35.db_ref, ...), custom_call_target="tpu_custom_call" | custom-call | tf_op jit(solution)/shard_map/pooling_step/pallas_call | solution.py:514
  93.9 6.2 %outputs.1 = (f32[1,1]{1,0:T(1,128)}, f32[7,7,768]{2,1,0:T(8,128)}, f32[1,768]{1,0:T(1,128)S(1)}, f32[768,256]{1,0:T(8,128)}, f32[1,256]{1,0:T(1,128)}, /*index=5*/f32[10,256,256]{2,1,0:T(8,128)}, f32[1,10]{1,0:T(1,128)}) custom-call(bf16[16,48,256]{2,1,0:T(8,128)(2,1)S(1)} %get-tuple-element.18.wg, bf16[16,8,384]{2,1,0:T(8,128)(2,1)S(1)} %get-tuple-element.19.dg, ...), custom_call_target="tpu_custom_call" | custom-call | tf_op jit(solution)/shard_map/outputs/pallas_call | solution.py:534
  100.1 0.6 reduce
Async XLA Ops:
  2.0 1.3 %copy-start = (bf16[10,256,256]{2,1,0:T(8,128)(2,1)S(1)}, bf16[10,256,256]{2,1,0:T(8,128)(2,1)}, u32[]{:S(2)}) copy-start(bf16[10,256,256]{2,1,0:T(8,128)(2,1)} %cw_ref.1) | copy-start | bytes 3932164
  3.3 1.0 copy-start.1
  4.3 0.9 copy-start.2
  5.2 0.7 copy-start.3
  5.9 0.7 copy-start.4

commit v2 on v1

--- a/solution.py
+++ b/solution.py
@@ -44,14 +44,16 @@
 
 
 def main_kernel(
-    x_ref, w_ref, db_ref, rw_ref, rb_ref, cw_ref, cb_ref, lab_ref,
-    wg_out, dg_out, root_out, small_out,
-    image, conv32, conv, before, feat, pre, cgrad,
+    x_hbm, w_hbm, db_hbm, rw_hbm, rb_hbm, cw_hbm, cb_hbm, lab_ref,
+    wg_out, dg_out, small_out, class_hbm,
+    class_out,
+    x_ref, w_ref, db_ref, rw_ref, rb_ref, cw_ref, cb_ref, root_out, factors,
+    image, border, conv, before, feat, pre, cgrad,
     csend, ksend, hrow, hcol, hcor,
     gram, grecv, gfull, colsum, crecv,
     ys, zs, ts, sym, mean_term,
     wsend, wrecv, wx, depth, dsend, drecv, dx,
-    halo_send, halo_recv, g_send, g_recv, c_send, c_recv, a_send, a_recv,
+    in_sem, out_sem, halo_send, halo_recv, g_send, g_recv, c_send, c_recv, a_send, a_recv,
     x_send, x_recv, s_send, s_recv, w_send, w_recv, wx_send, wx_recv, wa_send, wa_recv,
     d_send, d_recv, dx_send, dx_recv, da_send, da_recv,
 ):
@@ -82,11 +84,26 @@
     for offset in range(1, 8):
         pl.semaphore_signal(barrier, inc=1, device_id=line(offset)[0], device_id_type=MESH)
 
+    loads = [
+        pltpu.make_async_copy(src, dst, in_sem.at[i])
+        for i, (src, dst) in enumerate([
+            (x_hbm.at[0], x_ref), (w_hbm, w_ref), (db_hbm, db_ref), (rw_hbm, rw_ref),
+            (rb_hbm, rb_ref), (cw_hbm, cw_ref), (cb_hbm, cb_ref),
+        ])
+    ]
+    for load in loads:
+        load.start()
+    loads[0].wait()
+
     def fill(tile, carry):
         lanes = lanes_of(tile)
+        blank = jnp.zeros((8, 128), f32)
         for row in range(ROWS):
             start = (row + 3) * PITCH + BLOCK0
-            image[tile, start : start + COLS, :] = x_ref[0, row, :, lanes].astype(f32)
+            image[tile, start : start + COLS, :] = x_ref[row, :, lanes].astype(f32)
+            image[tile, start - 8 : start, :] = blank
+            image[tile, start + COLS : start + COLS + 8, :] = blank
+            border[tile, row * 32 : row * 32 + 32, :] = jnp.zeros((32, 128), f32)
         for side in range(2):
             for col in range(3):
                 at = BLOCK0 + col + (0 if side == 0 else COLS - 3)
@@ -97,13 +114,42 @@
         return carry
 
     lax.fori_loop(0, TILES, fill, 0)
+    loads[1].wait()
+    loads[2].wait()
+
+    def taps_of(lanes, b):
+        return [jnp.broadcast_to(w_ref[a, pl.ds(b, 1), lanes], (8, 128)) for a in range(KERNEL)]
+
+    def accumulate(acc, x, row, taps):
+        for a in range(KERNEL):
+            if 0 <= row - a < ROWS:
+                acc[row - a] = acc[row - a] + x * taps[a]
+
+    def conv_tile(tile, carry):
+        lanes = lanes_of(tile)
+
+        def group(jg, inner):
+            acc = [jnp.broadcast_to(db_ref[lanes].reshape(1, 128), (8, 128))] * ROWS
+            for b in range(KERNEL):
+                taps = taps_of(lanes, b)
+                for row in range(3, ROWS + 3):
+                    x = image[tile, pl.ds(jg * 8 + (row * PITCH + BLOCK0 - 3 + b), 8), :]
+                    accumulate(acc, x, row, taps)
+            for row in range(ROWS):
+                cgrad[tile, pl.ds(pl.multiple_of(jg * 8 + row * COLS, 8), 8), :] = acc[row]
+            return inner
+
+        lax.fori_loop(0, COLS // 8, group, 0)
+        return carry
+
+    lax.fori_loop(0, 2, conv_tile, 0)
     pl.semaphore_wait(barrier, 22)
 
     up, down = lax.rem(iz + 3, 4), lax.rem(iz + 1, 4)
     left, right = lax.rem(iy + 3, 4), lax.rem(iy + 1, 4)
     halo = [
-        (x_ref.at[0, pl.ds(ROWS - 3, 3)], hrow.at[0], (idp, down, iy)),
-        (x_ref.at[0, pl.ds(0, 3)], hrow.at[1], (idp, up, iy)),
+        (x_ref.at[pl.ds(ROWS - 3, 3)], hrow.at[0], (idp, down, iy)),
+        (x_ref.at[pl.ds(0, 3)], hrow.at[1], (idp, up, iy)),
         (csend.at[1], hcol.at[0], (idp, iz, right)),
         (csend.at[0], hcol.at[1], (idp, iz, left)),
         (ksend.at[3], hcor.at[0], (idp, down, right)),
@@ -117,6 +163,7 @@
     ]
     for copy in copies:
         copy.start()
+    lax.fori_loop(2, TILES, conv_tile, 0)
     for copy in copies:
         copy.wait()
     has_up, has_down, has_left, has_right = iz > 0, iz < 3, iy > 0, iy < 3
@@ -134,45 +181,56 @@
             for col in range(3):
                 at = BLOCK0 - 3 + col + side * (COLS + 3)
                 strip = hcol[side, col, :, lanes].astype(f32)
-                image[tile, pl.ds(3 * PITCH + at, ROWS, stride=PITCH), :] = jnp.where(
-                    has_col, strip, 0.0
-                )
+                strip = jnp.where(has_col, strip, 0.0)
+                image[tile, pl.ds(3 * PITCH + at, ROWS, stride=PITCH), :] = strip
+                spot = 21 + col if side == 0 else 8 + col
+                border[tile, pl.ds(spot, ROWS, stride=32), :] = strip
                 for end in range(2):
                     has_both = jnp.logical_and((has_up, has_down)[end], has_col)
                     strip = hcor[end * 2 + side, col, :, lanes].astype(f32)
                     strip = jnp.where(has_both, strip, 0.0)
                     strip = strip[5:8] if end == 0 else strip[0:3]
                     image[tile, pl.ds(19 * end * PITCH + at, 3, stride=PITCH), :] = strip
+
+        def load_rows(start, rows):
+            return {
+                row: cgrad[tile, pl.ds(pl.multiple_of(start + row * COLS, 8), 8), :] for row in rows
+            }
+
+        def store_rows(start, acc):
+            for row, value in acc.items():
+                cgrad[tile, pl.ds(pl.multiple_of(start + row * COLS, 8), 8), :] = value
+
+        def group(jg, inner):
+            acc = load_rows(jg * 8, (0, 1, 2, 13, 14, 15))
+            for b in range(KERNEL):
+                taps = taps_of(lanes, b)
+                for row in (0, 1, 2, 19, 20, 21):
+                    x = image[tile, pl.ds(jg * 8 + (row * PITCH + BLOCK0 - 3 + b), 8), :]
+                    accumulate(acc, x, row, taps)
+            store_rows(jg * 8, acc)
+            return inner
+
+        lax.fori_loop(0, COLS // 8, group, 0)
+        for side in range(2):
+            acc = load_rows(side * (COLS - 8), range(ROWS))
+            for b in (range(3), range(4, 7))[side]:
+                taps = taps_of(lanes, b)
+                for row in range(ROWS):
+                    spot = row * 32 + (21 + b if side == 0 else b - 3)
+                    accumulate(acc, border[tile, spot : spot + 8, :], row + 3, taps)
+            store_rows(side * (COLS - 8), acc)
+        conv[:, lanes] = cgrad[tile].astype(bf16)
         return carry
 
     lax.fori_loop(0, TILES, edges, 0)
 
-    def conv_tile(tile, carry):
-        lanes = lanes_of(tile)
-
-        def group(jg, inner):
-            acc = [jnp.broadcast_to(db_ref[:, lanes], (8, 128))] * ROWS
-            for b in range(KERNEL):
-                taps = [jnp.broadcast_to(w_ref[a, pl.ds(b, 1), lanes], (8, 128)) for a in range(KERNEL)]
-                for row in range(ROWS + 6):
-                    x = image[tile, pl.ds(jg * 8 + (row * PITCH + BLOCK0 - 3 + b), 8), :]
-                    for a in range(KERNEL):
-                        if 0 <= row - a < ROWS:
-                            acc[row - a] = acc[row - a] + x * taps[a]
-            for row in range(ROWS):
-                conv32[pl.ds(pl.multiple_of(jg * 8 + row * COLS, 8), 8), :] = acc[row]
-            return inner
-
-        lax.fori_loop(0, COLS // 8, group, 0)
-        conv[:, lanes] = conv32[...].astype(bf16)
-        return carry
-
-    lax.fori_loop(0, TILES, conv_tile, 0)
-
     colsum[...] = jnp.zeros_like(colsum)
+    loads[3].wait()
+    loads[4].wait()
     for part in range(4):
         rows = pl.ds(part * 256, 256)
-        value = jnp.dot(conv[rows, :], rw_ref[...], preferred_element_type=f32) + rb_ref[...]
+        value = jnp.dot(conv[rows, :], rw_ref[...], preferred_element_type=f32) + rb_ref[...].reshape(1, REDUCED)
         before[rows, :] = value
         active = (value / (1.0 + jnp.exp(-value))).astype(bf16)
         feat[rows, :] = active
@@ -250,8 +308,10 @@
     root = root_scale * last
     root_out[idp] = root.astype(bf16)
 
+    loads[5].wait()
+    loads[6].wait()
     class_id = lax.broadcasted_iota(jnp.int32, (1, CLASSES), 1)
-    logits = cb_ref[...]
+    logits = cb_ref[...].reshape(1, CLASSES)
     for k in range(CLASSES):
         weighted = jnp.sum(cw_ref[k].astype(f32) * root, axis=0, keepdims=True)
         logits = logits + jnp.where(class_id == k, jnp.sum(weighted, axis=1, keepdims=True), 0.0)
@@ -402,6 +462,31 @@
         d_copies.append(send(dsend.at[index], drecv.at[offset], d_send.at[offset], d_recv.at[offset], device))
     for copy in d_copies:
         copy.start()
+
+    for offset in range(1, 8):
+        _, source = line(offset, -1)
+        device = line(offset)[0]
+        send(root_out.at[source], root_out.at[source], x_send.at[offset], x_recv.at[offset], device).wait_recv()
+        send(small_out.at[source], small_out.at[source], s_send.at[offset], s_recv.at[offset], device).wait_recv()
+    for index in range(8):
+        for k in range(CLASSES):
+            factors[index * CLASSES + k] = jnp.broadcast_to(small_out[index, 0:1, k : k + 1], (8, 128))
+
+    def class_rows(block, carry):
+        rows = pl.ds(pl.multiple_of(block * 16, 16), 16)
+        for half in range(2):
+            lanes = slice(half * 128, half * 128 + 128)
+            blocks = [root_out[index, rows, lanes].astype(f32).reshape(2, 8, 128) for index in range(8)]
+            for k in range(CLASSES):
+                total = blocks[0] * factors[k]
+                for index in range(1, 8):
+                    total = total + blocks[index] * factors[index * CLASSES + k]
+                class_out[k, rows, lanes] = total.reshape(16, 128)
+        return carry
+
+    lax.fori_loop(0, 16, class_rows, 0)
+    store = pltpu.make_async_copy(class_out, class_hbm, out_sem)
+    store.start()
     for copy in d_copies:
         copy.wait()
     d_sum = dsend[me].astype(f32)
@@ -434,39 +519,38 @@
         device = plane(offset)[0]
         send(wg_out.at[source], wg_out.at[source], wa_send.at[offset], wa_recv.at[offset], device).wait_recv()
         send(dg_out.at[source], dg_out.at[source], da_send.at[offset], da_recv.at[offset], device).wait_recv()
-    for offset in range(1, 8):
-        _, source = line(offset, -1)
-        device = line(offset)[0]
-        send(root_out.at[source], root_out.at[source], x_send.at[offset], x_recv.at[offset], device).wait_recv()
-        send(small_out.at[source], small_out.at[source], s_send.at[offset], s_recv.at[offset], device).wait_recv()
     for copy in wa_copies + da_copies + roots + smalls:
         copy.wait_send()
-
-
-def finish_kernel(wg, dg, roots, smalls, loss, depth_grad, depth_bias, weight, bias, class_weight, class_bias):
-    k = pl.program_id(0)
-    lane = lax.broadcasted_iota(jnp.int32, (1, 128), 1)
-    total = jnp.zeros((REDUCED, REDUCED), f32)
-    for image in range(8):
-        factor = jnp.sum(jnp.where(lane == k, smalls[image, 0:1, :], 0.0), axis=1, keepdims=True)
-        total = total + factor * roots[image].astype(f32)
-    class_weight[0] = total
-
-    @pl.when(k == 0)
-    def _():
-        weight[...] = wg[...].astype(f32).reshape(CHANNELS, REDUCED)
-        for half in range(2):
-            lanes = slice(half * 384, half * 384 + 384)
-            for a in range(KERNEL):
-                depth_grad[a, :, lanes] = dg[a * 2 + half, 0:7, :].astype(f32)
-            depth_bias[:, lanes] = dg[half, 7:8, :].astype(f32)
-        bias[:, 0:128] = dg[2, 7:8, 0:128].astype(f32)
-        bias[:, 128:256] = dg[2, 7:8, 128:256].astype(f32)
-        small = smalls[0]
-        for image in range(1, 8):
-            small = small + smalls[image]
-        class_bias[...] = small[0:1, 0:CLASSES]
-        loss[...] = small[1:2, 0:1] * (1.0 / 8)
+    store.wait()
+
+
+def finish_kernel(
+    wg_hbm, dg_hbm, smalls_hbm, grads, loss, depth_grad, depth_bias, weight, bias, class_weight, class_bias,
+    wg, dg, smalls, sem,
+):
+    copy = pltpu.make_async_copy(grads, class_weight, sem.at[0])
+    copy.start()
+    loads = [
+        pltpu.make_async_copy(src, dst, sem.at[i + 1])
+        for i, (src, dst) in enumerate([(wg_hbm, wg), (dg_hbm, dg), (smalls_hbm, smalls)])
+    ]
+    for load in loads:
+        load.start()
+    for load in loads:
+        load.wait()
+    weight[...] = wg[...].astype(f32).reshape(CHANNELS, REDUCED)
+    for half in range(2):
+        lanes = slice(half * 384, half * 384 + 384)
+        for a in range(KERNEL):
+            depth_grad[a, :, lanes] = dg[a * 2 + half, 0:7, :].astype(f32)
+        depth_bias[lanes] = dg[half, 7:8, :].astype(f32).reshape(384)
+    bias[...] = dg[2, 7:8, 0:REDUCED].astype(f32).reshape(REDUCED)
+    small = smalls[0]
+    for image in range(1, 8):
+        small = small + smalls[image]
+    class_bias[...] = small[0:1, 0:CLASSES].reshape(CLASSES)
+    loss[...] = small[1:2, 0:1] * (1.0 / 8)
+    copy.wait()
 
 
 def body(
@@ -475,9 +559,20 @@
     vmem = pl.BlockSpec(memory_space=pltpu.VMEM)
     smem = pl.BlockSpec(memory_space=pltpu.SMEM)
     dma = pltpu.SemaphoreType.DMA
+    hbm = pl.BlockSpec(memory_space=pltpu.HBM)
     scratch = [
+        pltpu.VMEM((CLASSES, REDUCED, REDUCED), f32),
+        pltpu.VMEM((ROWS, COLS, CHANNELS), bf16),
+        pltpu.VMEM((KERNEL, KERNEL, CHANNELS), f32),
+        pltpu.VMEM((CHANNELS,), f32),
+        pltpu.VMEM((CHANNELS, REDUCED), bf16),
+        pltpu.VMEM((REDUCED,), f32),
+        pltpu.VMEM((CLASSES, REDUCED, REDUCED), bf16),
+        pltpu.VMEM((CLASSES,), f32),
+        pltpu.VMEM((8, REDUCED, REDUCED), bf16),
+        pltpu.VMEM((8 * CLASSES, 8, 128), f32),
         pltpu.VMEM((TILES, (ROWS + 6) * PITCH, 128), f32),
-        pltpu.VMEM((ROWS * COLS, 128), f32),
+        pltpu.VMEM((TILES, ROWS * 32, 128), f32),
         pltpu.VMEM((ROWS * COLS, CHANNELS), bf16),
         pltpu.VMEM((ROWS * COLS, REDUCED), f32),
         pltpu.VMEM((ROWS * COLS, REDUCED), bf16),
@@ -505,56 +600,51 @@
         pltpu.VMEM((16, 8, 384), bf16),
         pltpu.VMEM((16, 8, 384), bf16),
         pltpu.VMEM((8, 8, 384), bf16),
-        dma((8,)), dma((8,)),
+        dma((7,)), dma, dma((8,)), dma((8,)),
         dma((16,)), dma((16,)), dma((16,)), dma((16,)), dma((16,)), dma((16,)),
         dma((8,)), dma((8,)), dma((8,)), dma((8,)),
         dma((16,)), dma((16,)), dma((8,)), dma((8,)), dma((16,)), dma((16,)),
         dma((16,)), dma((16,)), dma((8,)), dma((8,)), dma((16,)), dma((16,)),
     ]
-    wg, dg, roots, smalls = pl.pallas_call(
+    partial = pl.pallas_call(
         main_kernel,
         out_shape=(
             jax.ShapeDtypeStruct((16, 48, REDUCED), bf16),
             jax.ShapeDtypeStruct((16, 8, 384), bf16),
-            jax.ShapeDtypeStruct((8, REDUCED, REDUCED), bf16),
             jax.ShapeDtypeStruct((8, 8, 128), f32),
+            jax.ShapeDtypeStruct((CLASSES, REDUCED, REDUCED), f32),
         ),
-        in_specs=[vmem] * 7 + [smem],
-        out_specs=(vmem,) * 4,
+        in_specs=[hbm] * 7 + [smem],
+        out_specs=(vmem,) * 3 + (hbm,),
         scratch_shapes=scratch,
         compiler_params=pltpu.CompilerParams(
-            collective_id=0, has_side_effects=True, vmem_limit_bytes=50 << 20
+            collective_id=0, has_side_effects=True, vmem_limit_bytes=63 << 20
         ),
         name="pooling_step",
     )(
-        features, depth_weight, depth_bias.reshape(1, CHANNELS), reduce_weight,
-        reduce_bias.reshape(1, REDUCED), class_weight, class_bias.reshape(1, CLASSES), labels,
+        features, depth_weight, depth_bias, reduce_weight, reduce_bias, class_weight, class_bias, labels
     )
-    whole = lambda *shape: pl.BlockSpec(shape, lambda k: (0,) * len(shape))
-    loss, depth_grad, depth_bias_grad, weight_grad, bias_grad, class_grad, class_bias_grad = pl.pallas_call(
+    loss, *grads = pl.pallas_call(
         finish_kernel,
-        grid=(CLASSES,),
         out_shape=(
             jax.ShapeDtypeStruct((1, 1), f32),
             jax.ShapeDtypeStruct((KERNEL, KERNEL, CHANNELS), f32),
-            jax.ShapeDtypeStruct((1, CHANNELS), f32),
+            jax.ShapeDtypeStruct((CHANNELS,), f32),
             jax.ShapeDtypeStruct((CHANNELS, REDUCED), f32),
-            jax.ShapeDtypeStruct((1, REDUCED), f32),
+            jax.ShapeDtypeStruct((REDUCED,), f32),
             jax.ShapeDtypeStruct((CLASSES, REDUCED, REDUCED), f32),
-            jax.ShapeDtypeStruct((1, CLASSES), f32),
+            jax.ShapeDtypeStruct((CLASSES,), f32),
         ),
-        in_specs=[whole(16, 48, REDUCED), whole(16, 8, 384), whole(8, REDUCED, REDUCED), whole(8, 8, 128)],
-        out_specs=(
-            whole(1, 1), whole(KERNEL, KERNEL, CHANNELS), whole(1, CHANNELS), whole(CHANNELS, REDUCED),
-            whole(1, REDUCED), pl.BlockSpec((1, REDUCED, REDUCED), lambda k: (k, 0, 0)), whole(1, CLASSES),
-        ),
-        compiler_params=pltpu.CompilerParams(vmem_limit_bytes=24 << 20),
+        in_specs=[hbm] * 4,
+        out_specs=(vmem,) * 5 + (hbm, vmem),
+        scratch_shapes=[
+            pltpu.VMEM((16, 48, REDUCED), bf16), pltpu.VMEM((16, 8, 384), bf16), pltpu.VMEM((8, 8, 128), f32),
+            dma((4,)),
+        ],
+        compiler_params=pltpu.CompilerParams(vmem_limit_bytes=63 << 20),
         name="outputs",
-    )(wg, dg, roots, smalls)
-    return (
-        loss.reshape(()), depth_grad, depth_bias_grad.reshape(CHANNELS), weight_grad,
-        bias_grad.reshape(REDUCED), class_grad, class_bias_grad.reshape(CLASSES),
-    )
+    )(*partial)
+    return (loss.reshape(()), *grads)
 
 
 def solution(mesh):

time: 101 us -> 162 us (1.60)
  Pallas kernels: 93.6 us -> 160 us
  local copies, waits for them, and re-layouts: 5.25 us -> 0 us
    pallas_call x1, Pallas kernels: 6.18 us -> 81.5 us  [body(): pl.pallas_call(finish_kernel, out_shape=(jax.ShapeDtypeStruct((1, 1), f32...]
    pallas_call x1, Pallas kernels: 87.4 us -> 78.7 us  [body(): pl.pallas_call(main_kernel, out_shape=(jax.ShapeDtypeStruct((16, 48, REDU...]
    unnamed x10 -> x0, local copies, waits for them, and re-layouts: 4.56 us -> none
where the time goes in v2:
time: 162 us
  Pallas kernels  160 us (99%)
    pallas_call x1, Pallas kernels, body(): pl.pallas_call(finish_kernel, out_shape=(jax.ShapeDtypeStruct((1, 1), f32...  81.5 us
    pallas_call x1, Pallas kernels, body(): pl.pallas_call(main_kernel, out_shape=(jax.ShapeDtypeStruct((16, 48, REDU...  78.7 us

profile of v2, /device:TPU:1, one launch (start us, length us, event | category | flops | bytes accessed | tf_op | source)
XLA Modules:
  0.0 161.5 jit_solution(5019941652831205257)
XLA Ops:
  1.3 78.7 %pooling_step.1 = (bf16[16,48,256]{2,1,0:T(8,128)(2,1)}, bf16[16,8,384]{2,1,0:T(8,128)(2,1)}, f32[8,8,128]{2,1,0:T(8,128)}, f32[10,256,256]{2,1,0:T(8,128)}) custom-call(bf16[1,16,64,768]{3,2,1,0:T(8,128)(2,1)} %x_hbm.1, f32[7,7,768]{2,1,0:T(8,128)} %w_hbm.1, f32[768]{0:T(1024)} %db_hbm.1, bf16[768,256]{1,0:T(8,128)(2,1)} %rw_hbm.1, f32[256]{0:T(256)} %rb_hbm.1, ...), custom_call_target="tpu_custom_call" | custom-call | tf_op jit(solution)/shard_map/pooling_step/pallas_call | solution.py:609
  80.0 81.5 %outputs.1 = (f32[1,1]{1,0:T(1,128)}, f32[7,7,768]{2,1,0:T(8,128)}, f32[768]{0:T(1024)}, f32[768,256]{1,0:T(8,128)}, f32[256]{0:T(256)}, /*index=5*/f32[10,256,256]{2,1,0:T(8,128)}, f32[10]{0:T(128)}) custom-call(bf16[16,48,256]{2,1,0:T(8,128)(2,1)} %get-tuple-element.18.wg_hbm, bf16[16,8,384]{2,1,0:T(8,128)(2,1)} %get-tuple-element.19.dg_hbm, ...), custom_call_target="tpu_custom_call" | custom-call | tf_op jit(solution)/shard_map/outputs/pallas_call | solution.py:627

commit v3 on v2

--- a/solution.py
+++ b/solution.py
@@ -50,7 +50,7 @@
     x_ref, w_ref, db_ref, rw_ref, rb_ref, cw_ref, cb_ref, root_out, factors,
     image, border, conv, before, feat, pre, cgrad,
     csend, ksend, hrow, hcol, hcor,
-    gram, grecv, gfull, colsum, crecv,
+    gram, grecv, square, gfull, colsum, crecv,
     ys, zs, ts, sym, mean_term,
     wsend, wrecv, wx, depth, dsend, drecv, dx,
     in_sem, out_sem, halo_send, halo_recv, g_send, g_recv, c_send, c_recv, a_send, a_recv,
@@ -147,9 +147,7 @@
 
     up, down = lax.rem(iz + 3, 4), lax.rem(iz + 1, 4)
     left, right = lax.rem(iy + 3, 4), lax.rem(iy + 1, 4)
-    halo = [
-        (x_ref.at[pl.ds(ROWS - 3, 3)], hrow.at[0], (idp, down, iy)),
-        (x_ref.at[pl.ds(0, 3)], hrow.at[1], (idp, up, iy)),
+    strips = [
         (csend.at[1], hcol.at[0], (idp, iz, right)),
         (csend.at[0], hcol.at[1], (idp, iz, left)),
         (ksend.at[3], hcor.at[0], (idp, down, right)),
@@ -157,15 +155,19 @@
         (ksend.at[1], hcor.at[2], (idp, up, right)),
         (ksend.at[0], hcor.at[3], (idp, up, left)),
     ]
-    copies = [
+    for part in range(3):
+        lanes = pl.ds(part * 256, 256)
+        strips += [
+            (x_ref.at[pl.ds(ROWS - 3, 3), :, lanes], hrow.at[0, :, :, lanes], (idp, down, iy)),
+            (x_ref.at[pl.ds(0, 3), :, lanes], hrow.at[1, :, :, lanes], (idp, up, iy)),
+        ]
+    halo = [
         send(src, dst, halo_send.at[i], halo_recv.at[i], device)
-        for i, (src, dst, device) in enumerate(halo)
+        for i, (src, dst, device) in enumerate(strips)
     ]
-    for copy in copies:
+    for copy in halo:
         copy.start()
     lax.fori_loop(2, TILES, conv_tile, 0)
-    for copy in copies:
-        copy.wait()
     has_up, has_down, has_left, has_right = iz > 0, iz < 3, iy > 0, iy < 3
 
     def edges(tile, carry):
@@ -223,7 +225,14 @@
         conv[:, lanes] = cgrad[tile].astype(bf16)
         return carry
 
-    lax.fori_loop(0, TILES, edges, 0)
+    for copy in halo[:6]:
+        copy.wait_recv()
+    for part in range(3):
+        for copy in halo[6 + 2 * part : 8 + 2 * part]:
+            copy.wait_recv()
+        lax.fori_loop(2 * part, 2 * part + 2, edges, 0)
+    for copy in halo:
+        copy.wait_send()
 
     colsum[...] = jnp.zeros_like(colsum)
     loads[3].wait()
@@ -255,27 +264,28 @@
     mine = gram[me]
     for offset in range(1, 16):
         mine = mine + grecv[offset]
-    gfull[me] = mine
-    gathers = []
-    for offset in range(1, 16):
-        device, _ = plane(offset)
-        gathers.append(send(gfull.at[me], gfull.at[me], a_send.at[offset], a_recv.at[offset], device))
-    for copy in gathers:
-        copy.start()
-    for copy in copies:
-        copy.wait_send()
-    for offset in range(1, 16):
-        _, source = plane(offset, -1)
-        send(gfull.at[source], gfull.at[source], a_send.at[offset], a_recv.at[offset], plane(offset)[0]).wait_recv()
-    for copy in gathers:
-        copy.wait_send()
-
     mean = crecv[0]
     for index in range(1, 16):
         mean = mean + crecv[index]
     mean = mean * (1.0 / count)
     wide = jnp.broadcast_to(mean, (REDUCED, REDUCED))
-    sigma = gfull[...].reshape(REDUCED, REDUCED) * (1.0 / count) - wide.T * wide
+    square[...] = (wide.T * wide).reshape(16, 16, REDUCED)
+    gfull[me] = (mine * (1.0 / count) - square[me]).astype(bf16)
+    gathers = []
+    for offset in range(1, 16):
+        device, _ = plane(offset)
+        gathers.append(send(gfull.at[me], gfull.at[me], a_send.at[offset], a_recv.at[offset], device))
+    for copy in gathers:
+        copy.start()
+    for copy in copies:
+        copy.wait_send()
+    for offset in range(1, 16):
+        _, source = plane(offset, -1)
+        send(gfull.at[source], gfull.at[source], a_send.at[offset], a_recv.at[offset], plane(offset)[0]).wait_recv()
+    for copy in gathers:
+        copy.wait_send()
+
+    sigma = gfull[...].reshape(REDUCED, REDUCED).astype(f32)
     row_id = lax.broadcasted_iota(jnp.int32, (REDUCED, REDUCED), 0)
     col_id = lax.broadcasted_iota(jnp.int32, (REDUCED, REDUCED), 1)
     diagonal = row_id == col_id
@@ -432,7 +442,21 @@
         wx_copies.append(send(wx.at[idp], wx.at[idp], wx_send.at[offset], wx_recv.at[offset], device))
     for copy in wx_copies:
         copy.start()
-    lax.fori_loop(3, 5, depth_tile, 0)
+    lax.fori_loop(3, TILES, depth_tile, 0)
+
+    for group8 in range(8):
+        for half in range(2):
+            for third in range(3):
+                dsend[group8 * 2 + half, :, third * 128 : third * 128 + 128] = depth[
+                    half * 3 + third, group8 * 8 : group8 * 8 + 8, :
+                ].astype(bf16)
+    d_copies = []
+    for offset in range(1, 16):
+        device, index = plane(offset)
+        d_copies.append(send(dsend.at[index], drecv.at[offset], d_send.at[offset], d_recv.at[offset], device))
+    for copy in d_copies:
+        copy.start()
+
     for offset in range(1, 8):
         _, source = line(offset, -1)
         send(wx.at[source], wx.at[source], wx_send.at[offset], wx_recv.at[offset], line(offset)[0]).wait_recv()
@@ -447,20 +471,6 @@
         device, _ = plane(offset)
         wa_copies.append(send(wg_out.at[me], wg_out.at[me], wa_send.at[offset], wa_recv.at[offset], device))
     for copy in wa_copies:
-        copy.start()
-    lax.fori_loop(5, 6, depth_tile, 0)
-
-    for group8 in range(8):
-        for half in range(2):
-            for third in range(3):
-                dsend[group8 * 2 + half, :, third * 128 : third * 128 + 128] = depth[
-                    half * 3 + third, group8 * 8 : group8 * 8 + 8, :
-                ].astype(bf16)
-    d_copies = []
-    for offset in range(1, 16):
-        device, index = plane(offset)
-        d_copies.append(send(dsend.at[index], drecv.at[offset], d_send.at[offset], d_recv.at[offset], device))
-    for copy in d_copies:
         copy.start()
 
     for offset in range(1, 8):
@@ -525,20 +535,30 @@
 
 
 def finish_kernel(
-    wg_hbm, dg_hbm, smalls_hbm, grads, loss, depth_grad, depth_bias, weight, bias, class_weight, class_bias,
-    wg, dg, smalls, sem,
+    wg_hbm, dg_hbm, smalls_hbm, grads,
+    loss_hbm, depth_hbm, depth_bias_hbm, weight_hbm, bias_hbm, class_weight, class_bias_hbm,
+    wg, dg, smalls, buffer, loss, depth_grad, depth_bias, weight, bias, class_bias,
+    load_sem, store_sem, class_in, class_out,
 ):
-    copy = pltpu.make_async_copy(grads, class_weight, sem.at[0])
-    copy.start()
     loads = [
-        pltpu.make_async_copy(src, dst, sem.at[i + 1])
+        pltpu.make_async_copy(src, dst, load_sem.at[i])
         for i, (src, dst) in enumerate([(wg_hbm, wg), (dg_hbm, dg), (smalls_hbm, smalls)])
     ]
-    for load in loads:
+    fetches = [pltpu.make_async_copy(grads.at[k], buffer.at[k], class_in.at[k]) for k in range(CLASSES)]
+    stores = [pltpu.make_async_copy(buffer.at[k], class_weight.at[k], class_out.at[k]) for k in range(CLASSES)]
+    results = [
+        pltpu.make_async_copy(src, dst, store_sem.at[i])
+        for i, (src, dst) in enumerate([
+            (weight, weight_hbm), (depth_grad, depth_hbm), (depth_bias, depth_bias_hbm),
+            (bias, bias_hbm), (class_bias, class_bias_hbm), (loss, loss_hbm),
+        ])
+    ]
+    for load in loads + fetches:
         load.start()
     for load in loads:
         load.wait()
     weight[...] = wg[...].astype(f32).reshape(CHANNELS, REDUCED)
+    results[0].start()
     for half in range(2):
         lanes = slice(half * 384, half * 384 + 384)
         for a in range(KERNEL):
@@ -550,7 +570,13 @@
         small = small + smalls[image]
     class_bias[...] = small[0:1, 0:CLASSES].reshape(CLASSES)
     loss[...] = small[1:2, 0:1] * (1.0 / 8)
-    copy.wait()
+    for result in results[1:]:
+        result.start()
+    for fetch, store in zip(fetches, stores):
+        fetch.wait()
+        store.start()
+    for copy in results + stores:
+        copy.wait()
 
 
 def body(
@@ -586,6 +612,7 @@
         pltpu.VMEM((16, 16, REDUCED), f32),
         pltpu.VMEM((16, 16, REDUCED), f32),
         pltpu.VMEM((16, 16, REDUCED), f32),
+        pltpu.VMEM((16, 16, REDUCED), bf16),
         pltpu.VMEM((1, REDUCED), f32),
         pltpu.VMEM((16, 1, REDUCED), f32),
         pltpu.VMEM((NEWTON_STEPS, 2, REDUCED, REDUCED), bf16),
@@ -600,7 +627,7 @@
         pltpu.VMEM((16, 8, 384), bf16),
         pltpu.VMEM((16, 8, 384), bf16),
         pltpu.VMEM((8, 8, 384), bf16),
-        dma((7,)), dma, dma((8,)), dma((8,)),
+        dma((7,)), dma, dma((12,)), dma((12,)),
         dma((16,)), dma((16,)), dma((16,)), dma((16,)), dma((16,)), dma((16,)),
         dma((8,)), dma((8,)), dma((8,)), dma((8,)),
         dma((16,)), dma((16,)), dma((8,)), dma((8,)), dma((16,)), dma((16,)),
@@ -636,10 +663,13 @@
             jax.ShapeDtypeStruct((CLASSES,), f32),
         ),
         in_specs=[hbm] * 4,
-        out_specs=(vmem,) * 5 + (hbm, vmem),
+        out_specs=(hbm,) * 7,
         scratch_shapes=[
             pltpu.VMEM((16, 48, REDUCED), bf16), pltpu.VMEM((16, 8, 384), bf16), pltpu.VMEM((8, 8, 128), f32),
-            dma((4,)),
+            pltpu.VMEM((CLASSES, REDUCED, REDUCED), f32), pltpu.VMEM((1, 1), f32),
+            pltpu.VMEM((KERNEL, KERNEL, CHANNELS), f32), pltpu.VMEM((CHANNELS,), f32),
+            pltpu.VMEM((CHANNELS, REDUCED), f32), pltpu.VMEM((REDUCED,), f32), pltpu.VMEM((CLASSES,), f32),
+            dma((3,)), dma((6,)), dma((CLASSES,)), dma((CLASSES,)),
         ],
         compiler_params=pltpu.CompilerParams(vmem_limit_bytes=63 << 20),
         name="outputs",

time: 162 us -> 80.4 us (0.50)
  Pallas kernels: 160 us -> 78.9 us
    pallas_call x1, Pallas kernels: 81.5 us -> 3.76 us  [body(): pl.pallas_call(finish_kernel, out_shape=(jax.ShapeDtypeStruct((1, 1), f32...]
    pallas_call x1, Pallas kernels: 78.7 us -> 75.2 us  [body(): pl.pallas_call(main_kernel, out_shape=(jax.ShapeDtypeStruct((16, 48, REDU...]
where the time goes in v3:
time: 80.4 us; the launch traced here: 80.2 us
  Pallas kernels  78.9 us (98%)
  between operations  1.29 us (2%)
    pallas_call x1, Pallas kernels, body(): pl.pallas_call(main_kernel, out_shape=(jax.ShapeDtypeStruct((16, 48, REDU...  75.2 us
    pallas_call x1, Pallas kernels, body(): pl.pallas_call(finish_kernel, out_shape=(jax.ShapeDtypeStruct((1, 1), f32...  3.76 us

profile of v3, /device:TPU:1, one launch (start us, length us, event | category | flops | bytes accessed | tf_op | source)
XLA Modules:
  0.0 80.2 jit_solution(849616611273500687)
XLA Ops:
  1.3 75.2 %pooling_step.1 = (bf16[16,48,256]{2,1,0:T(8,128)(2,1)}, bf16[16,8,384]{2,1,0:T(8,128)(2,1)}, f32[8,8,128]{2,1,0:T(8,128)}, f32[10,256,256]{2,1,0:T(8,128)}) custom-call(bf16[1,16,64,768]{3,2,1,0:T(8,128)(2,1)} %x_hbm.1, f32[7,7,768]{2,1,0:T(8,128)} %w_hbm.1, f32[768]{0:T(1024)} %db_hbm.1, bf16[768,256]{1,0:T(8,128)(2,1)} %rw_hbm.1, f32[256]{0:T(256)} %rb_hbm.1, ...), custom_call_target="tpu_custom_call" | custom-call | tf_op jit(solution)/shard_map/pooling_step/pallas_call | solution.py:636
  76.5 3.8 %outputs.1 = (f32[1,1]{1,0:T(1,128)}, f32[7,7,768]{2,1,0:T(8,128)}, f32[768]{0:T(1024)}, f32[768,256]{1,0:T(8,128)}, f32[256]{0:T(256)}, /*index=5*/f32[10,256,256]{2,1,0:T(8,128)}, f32[10]{0:T(128)}) custom-call(bf16[16,48,256]{2,1,0:T(8,128)(2,1)} %get-tuple-element.18.wg_hbm, bf16[16,8,384]{2,1,0:T(8,128)(2,1)} %get-tuple-element.19.dg_hbm, ...), custom_call_target="tpu_custom_call" | custom-call | tf_op jit(solution)/shard_map/outputs/pallas_call | solution.py:654

commit v4 on v3

--- a/solution.py
+++ b/solution.py
@@ -33,6 +33,51 @@
     return high, (value - high.astype(f32)).astype(bf16)
 
 
+def plus(a, b):
+    return b if a is None else a if b is None else a + b
+
+
+def minus(a, b):
+    return a if b is None else 0.0 - b if a is None else a - b
+
+
+def part_rows(rows):
+    even, odd = rows[0::2], rows[1::2]
+    return [
+        odd,
+        [minus(a, b) for a, b in zip(even, odd)],
+        [minus(a, b) for a, b in zip(even[1:], odd)],
+    ]
+
+
+def part_taps(taps):
+    even, odd = taps[0::2], taps[1::2]
+    both = [plus(a, b) for a, b in zip(even, odd + [None] * (len(even) - len(odd)))]
+    return [both, even, odd]
+
+
+def part_outs(count):
+    return [(count + 1) // 2, (count + 1) // 2, count // 2]
+
+
+def join(parts, count):
+    shared, first, second = parts
+    return [plus(shared[i // 2], (first, second)[i % 2][i // 2]) for i in range(count)]
+
+
+def twice(part, value):
+    return [leaf for half in part(value) for leaf in part(half)]
+
+
+def join_twice(leaves, count):
+    halves = part_outs(count)
+    return join([join(leaves[3 * i : 3 * i + 3], halves[i]) for i in range(3)], count)
+
+
+LEAF_ROWS = 5
+LEAVES = 9
+
+
 def products(*pairs):
     left, right = [], []
     for (a_high, a_low), (b_high, b_low) in pairs:
@@ -48,7 +93,7 @@
     wg_out, dg_out, small_out, class_hbm,
     class_out,
     x_ref, w_ref, db_ref, rw_ref, rb_ref, cw_ref, cb_ref, root_out, factors,
-    image, border, conv, before, feat, pre, cgrad,
+    leaf_rows, leaf_values, leaf_taps, leaf_sums, image, border, conv, before, feat, pre, cgrad,
     csend, ksend, hrow, hcol, hcor,
     gram, grecv, square, gfull, colsum, crecv,
     ys, zs, ts, sym, mean_term,
@@ -104,6 +149,9 @@
             image[tile, start - 8 : start, :] = blank
             image[tile, start + COLS : start + COLS + 8, :] = blank
             border[tile, row * 32 : row * 32 + 32, :] = jnp.zeros((32, 128), f32)
+        for row in (0, 1, 2, 19, 20, 21):
+            image[tile, row * PITCH : row * PITCH + 8, :] = blank
+            image[tile, row * PITCH + PITCH - 8 : row * PITCH + PITCH, :] = blank
         for side in range(2):
             for col in range(3):
                 at = BLOCK0 + col + (0 if side == 0 else COLS - 3)
@@ -113,6 +161,33 @@
                     ksend[end * 2 + side, col, :, lanes] = strip[8 * end : 8 * end + 8].astype(bf16)
         return carry
 
+    def build_leaves(tile, group, present):
+        rows = [
+            image[tile, pl.ds(pl.multiple_of(group * 8 + row * PITCH, 8), 8), :] if row in present else None
+            for row in range(ROWS + 6)
+        ]
+        for leaf, values in enumerate(twice(part_rows, rows)):
+            for k, value in enumerate(values[:LEAF_ROWS]):
+                if value is not None:
+                    leaf_rows[tile, leaf, pl.ds(pl.multiple_of(group * 8 + k * PITCH, 8), 8), :] = value
+
+    own_rows = range(3, ROWS + 3)
+    own_leaves = twice(part_rows, [0.0 if row in own_rows else None for row in range(ROWS + 6)])
+
+    def fill_leaves(tile, carry):
+        for leaf, values in enumerate(own_leaves):
+            for k, value in enumerate(values[:LEAF_ROWS]):
+                if value is not None:
+                    leaf_rows[tile, leaf, k * PITCH : k * PITCH + 8, :] = jnp.zeros((8, 128), f32)
+                    leaf_rows[tile, leaf, k * PITCH + 72 : k * PITCH + 80, :] = jnp.zeros((8, 128), f32)
+
+        def group_leaves(group, inner):
+            build_leaves(tile, group, own_rows)
+            return inner
+
+        lax.fori_loop(1, 9, group_leaves, 0)
+        return carry
+
     lax.fori_loop(0, TILES, fill, 0)
     loads[1].wait()
     loads[2].wait()
@@ -127,22 +202,57 @@
 
     def conv_tile(tile, carry):
         lanes = lanes_of(tile)
-
-        def group(jg, inner):
-            acc = [jnp.broadcast_to(db_ref[lanes].reshape(1, 128), (8, 128))] * ROWS
-            for b in range(KERNEL):
-                taps = taps_of(lanes, b)
-                for row in range(3, ROWS + 3):
-                    x = image[tile, pl.ds(jg * 8 + (row * PITCH + BLOCK0 - 3 + b), 8), :]
-                    accumulate(acc, x, row, taps)
-            for row in range(ROWS):
-                cgrad[tile, pl.ds(pl.multiple_of(jg * 8 + row * COLS, 8), 8), :] = acc[row]
+        fill_leaves(tile, 0)
+        taps = twice(part_taps, [w_ref[a, :, lanes] for a in range(KERNEL)])
+        for leaf in range(LEAVES):
+            for beta, tap in enumerate(taps[leaf]):
+                leaf_taps[leaf, beta, 0:KERNEL, :] = tap
+        outs = twice(part_outs, ROWS)
+        filled = []
+        for leaf in range(LEAVES):
+            weights = [
+                [jnp.broadcast_to(leaf_taps[leaf, beta, b : b + 1, :], (8, 128)) for b in range(KERNEL)]
+                for beta in range(len(taps[leaf]))
+            ]
+            here = [k for k, v in enumerate(own_leaves[leaf][:LEAF_ROWS]) if v is not None]
+            filled.append([
+                True if any(i + beta in here for beta in range(len(taps[leaf]))) else None
+                for i in range(outs[leaf])
+            ])
+
+            def pair(index, inner, leaf=leaf, weights=weights, here=here):
+                for jg in (index * 2, index * 2 + 1):
+                    acc = [None] * outs[leaf]
+                    for b in range(KERNEL):
+                        for k in here:
+                            x = leaf_rows[tile, leaf, pl.ds(jg * 8 + (k * PITCH + BLOCK0 - 3 + b), 8), :]
+                            for beta in range(len(weights)):
+                                if 0 <= k - beta < outs[leaf]:
+                                    acc[k - beta] = plus(acc[k - beta], x * weights[beta][b])
+                    for i, value in enumerate(acc):
+                        if value is not None:
+                            leaf_values[leaf, pl.ds(pl.multiple_of(jg * 8 + i * COLS, 8), 8), :] = value
+                return inner
+
+            lax.fori_loop(0, COLS // 16, pair, 0)
+
+        def combine(jg, inner):
+            bias = jnp.broadcast_to(db_ref[lanes].reshape(1, 128), (8, 128))
+            leaves = [
+                [
+                    leaf_values[leaf, pl.ds(pl.multiple_of(jg * 8 + i * COLS, 8), 8), :] if here else None
+                    for i, here in enumerate(filled[leaf])
+                ]
+                for leaf in range(LEAVES)
+            ]
+            for row, value in enumerate(join_twice(leaves, ROWS)):
+                cgrad[tile, pl.ds(pl.multiple_of(jg * 8 + row * COLS, 8), 8), :] = value + bias
             return inner
 
-        lax.fori_loop(0, COLS // 8, group, 0)
+        lax.fori_loop(0, COLS // 8, combine, 0)
         return carry
 
-    lax.fori_loop(0, 2, conv_tile, 0)
+    lax.fori_loop(0, 1, conv_tile, 0)
     pl.semaphore_wait(barrier, 22)
 
     up, down = lax.rem(iz + 3, 4), lax.rem(iz + 1, 4)
@@ -167,7 +277,7 @@
     ]
     for copy in halo:
         copy.start()
-    lax.fori_loop(2, TILES, conv_tile, 0)
+    lax.fori_loop(1, TILES, conv_tile, 0)
     has_up, has_down, has_left, has_right = iz > 0, iz < 3, iy > 0, iy < 3
 
     def edges(tile, carry):
@@ -257,6 +367,16 @@
         copies.append(send(colsum, crecv.at[me], c_send.at[offset], c_recv.at[offset], device))
     for copy in copies:
         copy.start()
+
+    def all_leaves(tile, carry):
+        def group_leaves(group, inner):
+            build_leaves(tile, group, range(ROWS + 6))
+            return inner
+
+        return lax.fori_loop(0, PITCH // 8, group_leaves, carry)
+
+    lax.fori_loop(0, TILES, all_leaves, 0)
+    leaf_sums[...] = jnp.zeros_like(leaf_sums)
     for offset in range(1, 16):
         _, source = plane(offset, -1)
         send(gram.at[0], grecv.at[offset], g_send.at[offset], g_recv.at[offset], plane(offset)[0]).wait_recv()
@@ -400,35 +520,49 @@
         copy.start()
 
     def depth_tile(tile, carry):
-        for b in range(KERNEL):
-
-            def group(jg, acc):
+        def grads(jg, inner):
+            rows = [
+                cgrad[tile, pl.ds(pl.multiple_of(jg * 8 + row * COLS, 8), 8), :] for row in range(ROWS)
+            ]
+            for leaf, values in enumerate(twice(part_taps, rows)):
+                for k, value in enumerate(values):
+                    leaf_values[leaf, pl.ds(pl.multiple_of(jg * 8 + k * COLS, 8), 8), :] = value
+            return inner
+
+        lax.fori_loop(0, COLS // 8, grads, 0)
+        outs = twice(part_outs, KERNEL)
+        zero = jnp.zeros((8, 128), f32)
+        for leaf in range(LEAVES):
+            count_out = outs[leaf]
+
+            def group(jg, acc, leaf=leaf, count_out=count_out):
                 acc = list(acc)
-                grads = [
-                    cgrad[tile, pl.ds(pl.multiple_of(jg * 8 + row * COLS, 8), 8), :]
-                    for row in range(ROWS)
+                taps = [
+                    leaf_values[leaf, pl.ds(pl.multiple_of(jg * 8 + k * COLS, 8), 8), :] for k in range(4)
                 ]
-                for row in range(ROWS + 6):
-                    x = image[tile, pl.ds(jg * 8 + (row * PITCH + BLOCK0 - 3 + b), 8), :]
-                    for a in range(KERNEL):
-                        if 0 <= row - a < ROWS:
-                            acc[a] = acc[a] + x * grads[row - a]
-                if b == 0:
-                    partial = grads[0]
-                    for row in range(1, ROWS):
-                        partial = partial + grads[row]
-                    acc[KERNEL] = acc[KERNEL] + partial
+                for b in range(KERNEL):
+                    for k in range(count_out + 3):
+                        x = leaf_rows[tile, leaf, pl.ds(jg * 8 + (k * PITCH + BLOCK0 - 3 + b), 8), :]
+                        for i in range(count_out):
+                            if 0 <= k - i < 4:
+                                acc[b * count_out + i] = acc[b * count_out + i] + x * taps[k - i]
+                if leaf == 0:
+                    acc[-1] = acc[-1] + ((taps[0] + taps[1]) + (taps[2] + taps[3]))
                 return tuple(acc)
 
-            zero = jnp.zeros((8, 128), f32)
-            sums = lax.fori_loop(0, COLS // 8, group, (zero,) * (KERNEL + (b == 0)))
-            for a in range(KERNEL):
-                depth[tile, a * 8 + b : a * 8 + b + 1, :] = jnp.sum(sums[a], axis=0, keepdims=True)
-            if b == 0:
-                depth[tile, 7:8, :] = jnp.sum(sums[KERNEL], axis=0, keepdims=True)
+            sums = lax.fori_loop(0, COLS // 8, group, (zero,) * (KERNEL * count_out + (leaf == 0)))
+            for b in range(KERNEL):
+                for i in range(count_out):
+                    leaf_sums[leaf, i, b : b + 1, :] = jnp.sum(sums[b * count_out + i], axis=0, keepdims=True)
+            if leaf == 0:
+                total = jnp.sum(sums[-1], axis=0, keepdims=True)
+        leaves = [[leaf_sums[leaf, i] for i in range(outs[leaf])] for leaf in range(LEAVES)]
+        for a, value in enumerate(join_twice(leaves, KERNEL)):
+            depth[tile, a * 8 : a * 8 + 7, :] = value[0:7]
+        depth[tile, 7:8, :] = total
         return carry
 
-    lax.fori_loop(0, 3, depth_tile, 0)
+    lax.fori_loop(0, 5, depth_tile, 0)
 
     for copy in w_copies:
         copy.wait()
@@ -442,7 +576,7 @@
         wx_copies.append(send(wx.at[idp], wx.at[idp], wx_send.at[offset], wx_recv.at[offset], device))
     for copy in wx_copies:
         copy.start()
-    lax.fori_loop(3, TILES, depth_tile, 0)
+    lax.fori_loop(5, TILES, depth_tile, 0)
 
     for group8 in range(8):
         for half in range(2):
@@ -597,6 +731,10 @@
         pltpu.VMEM((CLASSES,), f32),
         pltpu.VMEM((8, REDUCED, REDUCED), bf16),
         pltpu.VMEM((8 * CLASSES, 8, 128), f32),
+        pltpu.VMEM((TILES, LEAVES, LEAF_ROWS * PITCH, 128), f32),
+        pltpu.VMEM((LEAVES, 4 * COLS, 128), f32),
+        pltpu.VMEM((LEAVES, 2, 8, 128), f32),
+        pltpu.VMEM((LEAVES, 2, 8, 128), f32),
         pltpu.VMEM((TILES, (ROWS + 6) * PITCH, 128), f32),
         pltpu.VMEM((TILES, ROWS * 32, 128), f32),
         pltpu.VMEM((ROWS * COLS, CHANNELS), bf16),

time: 80.4 us -> 76.6 us (0.953)
  Pallas kernels: 78.9 us -> 75.2 us
    pallas_call x1, Pallas kernels: 75.2 us -> 71.4 us  [body(): pl.pallas_call(main_kernel, out_shape=(jax.ShapeDtypeStruct((16, 48, REDU...]
where the time goes in v4:
time: 76.6 us; the launch traced here: 76.5 us
  Pallas kernels  75.2 us (98%)
  between operations  1.29 us (2%)
    pallas_call x1, Pallas kernels, body(): pl.pallas_call(main_kernel, out_shape=(jax.ShapeDtypeStruct((16, 48, REDU...  71.4 us
    pallas_call x1, Pallas kernels, body(): pl.pallas_call(finish_kernel, out_shape=(jax.ShapeDtypeStruct((1, 1), f32...  3.76 us

profile of v4, /device:TPU:1, one launch (start us, length us, event | category | flops | bytes accessed | tf_op | source)
XLA Modules:
  0.0 76.5 jit_solution(4125594678006673456)
XLA Ops:
  1.3 71.4 %pooling_step.1 = (bf16[16,48,256]{2,1,0:T(8,128)(2,1)}, bf16[16,8,384]{2,1,0:T(8,128)(2,1)}, f32[8,8,128]{2,1,0:T(8,128)}, f32[10,256,256]{2,1,0:T(8,128)}) custom-call(bf16[1,16,64,768]{3,2,1,0:T(8,128)(2,1)} %x_hbm.1, f32[7,7,768]{2,1,0:T(8,128)} %w_hbm.1, f32[768]{0:T(1024)} %db_hbm.1, bf16[768,256]{1,0:T(8,128)(2,1)} %rw_hbm.1, f32[256]{0:T(256)} %rb_hbm.1, ...), custom_call_target="tpu_custom_call" | custom-call | tf_op jit(solution)/shard_map/pooling_step/pallas_call | solution.py:774
  72.7 3.8 %outputs.1 = (f32[1,1]{1,0:T(1,128)}, f32[7,7,768]{2,1,0:T(8,128)}, f32[768]{0:T(1024)}, f32[768,256]{1,0:T(8,128)}, f32[256]{0:T(256)}, /*index=5*/f32[10,256,256]{2,1,0:T(8,128)}, f32[10]{0:T(128)}) custom-call(bf16[16,48,256]{2,1,0:T(8,128)(2,1)} %get-tuple-element.18.wg_hbm, bf16[16,8,384]{2,1,0:T(8,128)(2,1)} %get-tuple-element.19.dg_hbm, ...), custom_call_target="tpu_custom_call" | custom-call | tf_op jit(solution)/shard_map/outputs/pallas_call | solution.py:792

commit v5 on v4

--- a/solution.py
+++ b/solution.py
@@ -357,8 +357,12 @@
     total = lax.dot_general(
         feat[...], feat[...], (((0,), (0,)), ((), ())), preferred_element_type=f32
     )
-    gram[...] = total.reshape(16, 16, REDUCED)
-    crecv[me] = colsum[...]
+    own_mean = colsum[...] * (1.0 / (ROWS * COLS))
+    wide = jnp.broadcast_to(own_mean, (REDUCED, REDUCED))
+    centred = total * (1.0 / (ROWS * COLS)) - wide.T * wide
+    gram[...] = centred.astype(bf16).reshape(16, 16, REDUCED)
+    colsum[...] = own_mean
+    crecv[me] = own_mean
 
     copies = []
     for offset in range(1, 16):
@@ -381,16 +385,19 @@
         _, source = plane(offset, -1)
         send(gram.at[0], grecv.at[offset], g_send.at[offset], g_recv.at[offset], plane(offset)[0]).wait_recv()
         send(colsum, crecv.at[source], c_send.at[offset], c_recv.at[offset], plane(offset)[0]).wait_recv()
-    mine = gram[me]
-    for offset in range(1, 16):
-        mine = mine + grecv[offset]
     mean = crecv[0]
     for index in range(1, 16):
         mean = mean + crecv[index]
-    mean = mean * (1.0 / count)
-    wide = jnp.broadcast_to(mean, (REDUCED, REDUCED))
-    square[...] = (wide.T * wide).reshape(16, 16, REDUCED)
-    gfull[me] = (mine * (1.0 / count) - square[me]).astype(bf16)
+    mean = mean * (1.0 / 16)
+    between = split(crecv[...].reshape(16, REDUCED) - mean)
+    square[...] = sum(
+        lax.dot_general(a, b, (((0,), (0,)), ((), ())), preferred_element_type=f32)
+        for a, b in ((between[0], between[0]), (between[0], between[1]), (between[1], between[0]))
+    ).reshape(16, 16, REDUCED)
+    mine = gram[me].astype(f32) + square[me]
+    for offset in range(1, 16):
+        mine = mine + grecv[offset].astype(f32)
+    gfull[me] = (mine * (1.0 / 16)).astype(bf16)
     gathers = []
     for offset in range(1, 16):
         device, _ = plane(offset)
@@ -717,9 +724,9 @@
     features, depth_weight, depth_bias, reduce_weight, reduce_bias, class_weight, class_bias, labels
 ):
     vmem = pl.BlockSpec(memory_space=pltpu.VMEM)
-    smem = pl.BlockSpec(memory_space=pltpu.SMEM)
     dma = pltpu.SemaphoreType.DMA
     hbm = pl.BlockSpec(memory_space=pltpu.HBM)
+    smem = pl.BlockSpec(memory_space=pltpu.SMEM)
     scratch = [
         pltpu.VMEM((CLASSES, REDUCED, REDUCED), f32),
         pltpu.VMEM((ROWS, COLS, CHANNELS), bf16),
@@ -747,8 +754,8 @@
         pltpu.VMEM((2, 3, COLS, CHANNELS), bf16),
         pltpu.VMEM((2, 3, 16, CHANNELS), bf16),
         pltpu.VMEM((4, 3, 8, CHANNELS), bf16),
-        pltpu.VMEM((16, 16, REDUCED), f32),
-        pltpu.VMEM((16, 16, REDUCED), f32),
+        pltpu.VMEM((16, 16, REDUCED), bf16),
+        pltpu.VMEM((16, 16, REDUCED), bf16),
         pltpu.VMEM((16, 16, REDUCED), f32),
         pltpu.VMEM((16, 16, REDUCED), bf16),
         pltpu.VMEM((1, REDUCED), f32),

time: 76.6 us -> 75.6 us (0.987)
  Pallas kernels: 75.2 us -> 74.2 us
    pallas_call x1, Pallas kernels: 71.4 us -> 70.4 us  [body(): pl.pallas_call(main_kernel, out_shape=(jax.ShapeDtypeStruct((16, 48, REDU...]
where the time goes in v5:
time: 75.6 us; the launch traced here: 75.5 us
  Pallas kernels  74.2 us (98%)
  between operations  1.29 us (2%)
    pallas_call x1, Pallas kernels, body(): pl.pallas_call(main_kernel, out_shape=(jax.ShapeDtypeStruct((16, 48, REDU...  70.4 us
    pallas_call x1, Pallas kernels, body(): pl.pallas_call(finish_kernel, out_shape=(jax.ShapeDtypeStruct((1, 1), f32...  3.76 us

profile of v5, /device:TPU:1, one launch (start us, length us, event | category | flops | bytes accessed | tf_op | source)
XLA Modules:
  0.0 75.5 jit_solution(13104565308152072734)
XLA Ops:
  1.3 70.4 %pooling_step.1 = (bf16[16,48,256]{2,1,0:T(8,128)(2,1)}, bf16[16,8,384]{2,1,0:T(8,128)(2,1)}, f32[8,8,128]{2,1,0:T(8,128)}, f32[10,256,256]{2,1,0:T(8,128)}) custom-call(bf16[1,16,64,768]{3,2,1,0:T(8,128)(2,1)} %x_hbm.1, f32[7,7,768]{2,1,0:T(8,128)} %w_hbm.1, f32[768]{0:T(1024)} %db_hbm.1, bf16[768,256]{1,0:T(8,128)(2,1)} %rw_hbm.1, f32[256]{0:T(256)} %rb_hbm.1, ...), custom_call_target="tpu_custom_call" | custom-call | tf_op jit(solution)/shard_map/pooling_step/pallas_call | solution.py:781
  71.7 3.8 %outputs.1 = (f32[1,1]{1,0:T(1,128)}, f32[7,7,768]{2,1,0:T(8,128)}, f32[768]{0:T(1024)}, f32[768,256]{1,0:T(8,128)}, f32[256]{0:T(256)}, /*index=5*/f32[10,256,256]{2,1,0:T(8,128)}, f32[10]{0:T(128)}) custom-call(bf16[16,48,256]{2,1,0:T(8,128)(2,1)} %get-tuple-element.18.wg_hbm, bf16[16,8,384]{2,1,0:T(8,128)(2,1)} %get-tuple-element.19.dg_hbm, ...), custom_call_target="tpu_custom_call" | custom-call | tf_op jit(solution)/shard_map/outputs/pallas_call | solution.py:799

commit v6 on v5

--- a/solution.py
+++ b/solution.py
@@ -18,6 +18,8 @@
 CLASSES = 10
 PITCH = 80
 BLOCK0 = 8
+PLANE = sorted(range(1, 16), key=lambda o: -(min(o // 4, 4 - o // 4) + min(o % 4, 4 - o % 4)))
+LINE = sorted(range(1, 8), key=lambda o: -min(o, 8 - o))
 epsilon = 1e-05
 loss_scale = 64.0
 f32 = jnp.float32
@@ -364,11 +366,12 @@
     colsum[...] = own_mean
     crecv[me] = own_mean
 
-    copies = []
-    for offset in range(1, 16):
+    copies, means = [], []
+    for offset in PLANE:
         device, index = plane(offset)
         copies.append(send(gram.at[index], grecv.at[offset], g_send.at[offset], g_recv.at[offset], device))
-        copies.append(send(colsum, crecv.at[me], c_send.at[offset], c_recv.at[offset], device))
+        means.append(send(colsum, crecv.at[me], c_send.at[offset], c_recv.at[offset], device))
+    copies = means + copies
     for copy in copies:
         copy.start()
 
@@ -383,7 +386,6 @@
     leaf_sums[...] = jnp.zeros_like(leaf_sums)
     for offset in range(1, 16):
         _, source = plane(offset, -1)
-        send(gram.at[0], grecv.at[offset], g_send.at[offset], g_recv.at[offset], plane(offset)[0]).wait_recv()
         send(colsum, crecv.at[source], c_send.at[offset], c_recv.at[offset], plane(offset)[0]).wait_recv()
     mean = crecv[0]
     for index in range(1, 16):
@@ -394,16 +396,23 @@
         lax.dot_general(a, b, (((0,), (0,)), ((), ())), preferred_element_type=f32)
         for a, b in ((between[0], between[0]), (between[0], between[1]), (between[1], between[0]))
     ).reshape(16, 16, REDUCED)
+    for offset in PLANE:
+        send(gram.at[0], grecv.at[offset], g_send.at[offset], g_recv.at[offset], plane(offset)[0]).wait_recv()
     mine = gram[me].astype(f32) + square[me]
     for offset in range(1, 16):
         mine = mine + grecv[offset].astype(f32)
     gfull[me] = (mine * (1.0 / 16)).astype(bf16)
     gathers = []
-    for offset in range(1, 16):
+    for offset in PLANE:
         device, _ = plane(offset)
         gathers.append(send(gfull.at[me], gfull.at[me], a_send.at[offset], a_recv.at[offset], device))
     for copy in gathers:
         copy.start()
+    for part in range(4):
+        rows = pl.ds(part * 256, 256)
+        value = before[rows, :]
+        gate = 1.0 / (1.0 + jnp.exp(-value))
+        before[rows, :] = gate * (1.0 + value * (1.0 - gate))
     for copy in copies:
         copy.wait_send()
     for offset in range(1, 16):
@@ -460,7 +469,7 @@
     small_out[idp, 0:1, 0:CLASSES] = logit_grad
     small_out[idp, 1:2, :] = jnp.broadcast_to(loss, (1, 128))
     roots, smalls = [], []
-    for offset in range(1, 8):
+    for offset in LINE:
         device, _ = line(offset)
         roots.append(send(root_out.at[idp], root_out.at[idp], x_send.at[offset], x_recv.at[offset], device))
         smalls.append(send(small_out.at[idp], small_out.at[idp], s_send.at[offset], s_recv.at[offset], device))
@@ -502,9 +511,7 @@
     for part in range(4):
         rows = pl.ds(part * 256, 256)
         feat_grad = jnp.dot(feat[rows, :], sym[...], preferred_element_type=f32) - mean_term[0:1, :]
-        value = before[rows, :]
-        gate = 1.0 / (1.0 + jnp.exp(-value))
-        pre_grad = (feat_grad * gate * (1.0 + value * (1.0 - gate))).astype(bf16)
+        pre_grad = (feat_grad * before[rows, :]).astype(bf16)
         pre[rows, :] = pre_grad
         bias_grad = bias_grad + jnp.sum(pre_grad.astype(f32), axis=0, keepdims=True)
         conv_grad = lax.dot_general(
@@ -520,7 +527,7 @@
     depth[1, 15:16, :] = bias_grad[:, 128:256]
 
     w_copies = []
-    for offset in range(1, 16):
+    for offset in PLANE:
         device, index = plane(offset)
         w_copies.append(send(wsend.at[index], wrecv.at[offset], w_send.at[offset], w_recv.at[offset], device))
     for copy in w_copies:
@@ -578,7 +585,7 @@
         w_sum = w_sum + wrecv[offset].astype(f32)
     wx[idp] = w_sum.astype(bf16)
     wx_copies = []
-    for offset in range(1, 8):
+    for offset in LINE:
         device, _ = line(offset)
         wx_copies.append(send(wx.at[idp], wx.at[idp], wx_send.at[offset], wx_recv.at[offset], device))
     for copy in wx_copies:
@@ -592,7 +599,7 @@
                     half * 3 + third, group8 * 8 : group8 * 8 + 8, :
                 ].astype(bf16)
     d_copies = []
-    for offset in range(1, 16):
+    for offset in PLANE:
         device, index = plane(offset)
         d_copies.append(send(dsend.at[index], drecv.at[offset], d_send.at[offset], d_recv.at[offset], device))
     for copy in d_copies:
@@ -608,7 +615,7 @@
         w_sum = w_sum + wx[index].astype(f32)
     wg_out[me] = w_sum.astype(bf16)
     wa_copies = []
-    for offset in range(1, 16):
+    for offset in PLANE:
         device, _ = plane(offset)
         wa_copies.append(send(wg_out.at[me], wg_out.at[me], wa_send.at[offset], wa_recv.at[offset], device))
     for copy in wa_copies:
@@ -645,7 +652,7 @@
         d_sum = d_sum + drecv[offset].astype(f32)
     dx[idp] = d_sum.astype(bf16)
     dx_copies = []
-    for offset in range(1, 8):
+    for offset in LINE:
         device, _ = line(offset)
         dx_copies.append(send(dx.at[idp], dx.at[idp], dx_send.at[offset], dx_recv.at[offset], device))
     for copy in dx_copies:
@@ -660,7 +667,7 @@
         d_sum = d_sum + dx[index].astype(f32)
     dg_out[me] = d_sum.astype(bf16)
     da_copies = []
-    for offset in range(1, 16):
+    for offset in PLANE:
         device, _ = plane(offset)
         da_copies.append(send(dg_out.at[me], dg_out.at[me], da_send.at[offset], da_recv.at[offset], device))
     for copy in da_copies:
@@ -700,6 +707,9 @@
         load.wait()
     weight[...] = wg[...].astype(f32).reshape(CHANNELS, REDUCED)
     results[0].start()
+    for fetch, store in zip(fetches, stores):
+        fetch.wait()
+        store.start()
     for half in range(2):
         lanes = slice(half * 384, half * 384 + 384)
         for a in range(KERNEL):
@@ -713,9 +723,6 @@
     loss[...] = small[1:2, 0:1] * (1.0 / 8)
     for result in results[1:]:
         result.start()
-    for fetch, store in zip(fetches, stores):
-        fetch.wait()
-        store.start()
     for copy in results + stores:
         copy.wait()
 

time: 75.6 us -> 74.1 us (0.980)
  Pallas kernels: 74.2 us -> 72.7 us
    pallas_call x1, Pallas kernels: 70.4 us -> 68.9 us  [body(): pl.pallas_call(main_kernel, out_shape=(jax.ShapeDtypeStruct((16, 48, REDU...]
where the time goes in v6:
time: 74.1 us; the launch traced here: 74 us
  Pallas kernels  72.7 us (98%)
  between operations  1.29 us (2%)
    pallas_call x1, Pallas kernels, body(): pl.pallas_call(main_kernel, out_shape=(jax.ShapeDtypeStruct((16, 48, REDU...  68.9 us
    pallas_call x1, Pallas kernels, body(): pl.pallas_call(finish_kernel, out_shape=(jax.ShapeDtypeStruct((1, 1), f32...  3.76 us

profile of v6, /device:TPU:1, one launch (start us, length us, event | category | flops | bytes accessed | tf_op | source)
XLA Modules:
  0.0 74.0 jit_solution(13314347410562096785)
XLA Ops:
  1.3 68.9 %pooling_step.1 = (bf16[16,48,256]{2,1,0:T(8,128)(2,1)}, bf16[16,8,384]{2,1,0:T(8,128)(2,1)}, f32[8,8,128]{2,1,0:T(8,128)}, f32[10,256,256]{2,1,0:T(8,128)}) custom-call(bf16[1,16,64,768]{3,2,1,0:T(8,128)(2,1)} %x_hbm.1, f32[7,7,768]{2,1,0:T(8,128)} %w_hbm.1, f32[768]{0:T(1024)} %db_hbm.1, bf16[768,256]{1,0:T(8,128)(2,1)} %rw_hbm.1, f32[256]{0:T(256)} %rb_hbm.1, ...), custom_call_target="tpu_custom_call" | custom-call | tf_op jit(solution)/shard_map/pooling_step/pallas_call | solution.py:788
  70.2 3.8 %outputs.1 = (f32[1,1]{1,0:T(1,128)}, f32[7,7,768]{2,1,0:T(8,128)}, f32[768]{0:T(1024)}, f32[768,256]{1,0:T(8,128)}, f32[256]{0:T(256)}, /*index=5*/f32[10,256,256]{2,1,0:T(8,128)}, f32[10]{0:T(128)}) custom-call(bf16[16,48,256]{2,1,0:T(8,128)(2,1)} %get-tuple-element.18.wg_hbm, bf16[16,8,384]{2,1,0:T(8,128)(2,1)} %get-tuple-element.19.dg_hbm, ...), custom_call_target="tpu_custom_call" | custom-call | tf_op jit(solution)/shard_map/outputs/pallas_call | solution.py:806

commit v7 on v6

--- a/solution.py
+++ b/solution.py
@@ -749,7 +749,7 @@
         pltpu.VMEM((LEAVES, 4 * COLS, 128), f32),
         pltpu.VMEM((LEAVES, 2, 8, 128), f32),
         pltpu.VMEM((LEAVES, 2, 8, 128), f32),
-        pltpu.VMEM((TILES, (ROWS + 6) * PITCH, 128), f32),
+        pltpu.VMEM((TILES, (ROWS + 12) * PITCH, 128), f32),
         pltpu.VMEM((TILES, ROWS * 32, 128), f32),
         pltpu.VMEM((ROWS * COLS, CHANNELS), bf16),
         pltpu.VMEM((ROWS * COLS, REDUCED), f32),

time: 74.1 us -> 74.1 us (level)
  no operation moved by 1% of the time
where the time goes in v7:
time: 74.1 us; the launch traced here: 74 us
  Pallas kernels  72.7 us (98%)
  between operations  1.29 us (2%)
    pallas_call x1, Pallas kernels, body(): pl.pallas_call(main_kernel, out_shape=(jax.ShapeDtypeStruct((16, 48, REDU...  68.9 us
    pallas_call x1, Pallas kernels, body(): pl.pallas_call(finish_kernel, out_shape=(jax.ShapeDtypeStruct((1, 1), f32...  3.76 us

profile of v7, /device:TPU:1, one launch (start us, length us, event | category | flops | bytes accessed | tf_op | source)
XLA Modules:
  0.0 74.0 jit_solution(15897172868696553268)
XLA Ops:
  1.3 68.9 %pooling_step.1 = (bf16[16,48,256]{2,1,0:T(8,128)(2,1)}, bf16[16,8,384]{2,1,0:T(8,128)(2,1)}, f32[8,8,128]{2,1,0:T(8,128)}, f32[10,256,256]{2,1,0:T(8,128)}) custom-call(bf16[1,16,64,768]{3,2,1,0:T(8,128)(2,1)} %x_hbm.1, f32[7,7,768]{2,1,0:T(8,128)} %w_hbm.1, f32[768]{0:T(1024)} %db_hbm.1, bf16[768,256]{1,0:T(8,128)(2,1)} %rw_hbm.1, f32[256]{0:T(256)} %rb_hbm.1, ...), custom_call_target="tpu_custom_call" | custom-call | tf_op jit(solution)/shard_map/pooling_step/pallas_call | solution.py:788
  70.2 3.8 %outputs.1 = (f32[1,1]{1,0:T(1,128)}, f32[7,7,768]{2,1,0:T(8,128)}, f32[768]{0:T(1024)}, f32[768,256]{1,0:T(8,128)}, f32[256]{0:T(256)}, /*index=5*/f32[10,256,256]{2,1,0:T(8,128)}, f32[10]{0:T(128)}) custom-call(bf16[16,48,256]{2,1,0:T(8,128)(2,1)} %get-tuple-element.18.wg_hbm, bf16[16,8,384]{2,1,0:T(8,128)(2,1)} %get-tuple-element.19.dg_hbm, ...), custom_call_target="tpu_custom_call" | custom-call | tf_op jit(solution)/shard_map/outputs/pallas_call | solution.py:806
